TPU v7x, 1024 devices: a whole 4x8x16 slice. The times are simulated.
1024 devices in a mesh: dp: 4 (over x), seq: 16 (over y, core), heads: 16 (over z).
Axes of the slice: x: 4, y: 8, z: 16, core: 2. Of those that a mesh axis runs over, the one named last changes fastest.
Arguments:
- hidden: bfloat16 [4, 4096, 6144], P('dp', 'seq'), may hold values from -6 to 6
- w_gate: bfloat16 [6144, 4096], P('dp', 'heads'), may hold values from -0.078125 to 0.078125
- query_rows: bfloat16 [4, 4096, 4096], P('dp', 'seq', 'heads'), may hold values from -6 to 6
- key_rows: bfloat16 [4, 4096, 4096], P('dp', 'seq', 'heads'), may hold values from -6 to 6
- value_rows: bfloat16 [4, 4096, 4096], P('dp', 'seq', 'heads'), may hold values from -6 to 6
- target: bfloat16 [4, 4096, 4096], P('dp', 'seq', 'heads'), may hold values from -6 to 6
- decay_index: int32 [32], P('heads'), may hold values from 0 to 15
- loss_mask: int32 [4, 4096], P('dp', 'seq'), may hold values from 0 to 1
- doc_reset: int32 [4, 4096], P('dp', 'seq'), may hold values from 0 to 1, as said below
Outputs:
- gated_out: bfloat16 [4, 4096, 4096], P('dp', 'seq', 'heads')
- grad_gate: bfloat16 [4, 4096, 4096], P('dp', 'seq', 'heads')
- grad_query: bfloat16 [4, 4096, 4096], P('dp', 'seq', 'heads')
- grad_key: bfloat16 [4, 4096, 4096], P('dp', 'seq', 'heads')
- grad_value: bfloat16 [4, 4096, 4096], P('dp', 'seq', 'heads')
- mean_loss: float32 [], replicated
Inputs may be any that keep to these rules, and one draw needn't show every extreme that they name: `doc_reset`: at most three flags in each sequence.
All inputs are finite; a program needn't handle non-finite values.
Results may differ from a plain program's by a relative error of at most 0.0075.
Values may be sent and summed in bfloat16 or wider, within the bound.
A program may use at most 64 MiB of HBM per device.

v0:
```python
import functools

import jax
import jax.numpy as jnp
from jax import lax
from jax.sharding import Mesh
from jax.sharding import PartitionSpec as P

TABLE = 16
SEQ = ("seq_0", "seq_1")
DP_SEQ_HEADS = ("dp", "seq_0", "seq_1", "heads")


highest = lax.Precision.HIGHEST
norm_eps = 1e-06


def filled_with(value, identity):
    return jax.tree.map(
        lambda a, e: jnp.broadcast_to(jnp.asarray(e, a.dtype), a.shape), value, identity
    )


def entering(value, axes, combine, identity, reverse):
    before = start = filled_with(value, identity)
    total = value
    for axis in reversed(axes):
        count, position = (lax.axis_size(axis), lax.axis_index(axis))
        pieces = jax.tree.map(lambda part: lax.all_gather(part, axis), total)
        inside, total = (start, start)
        for k in reversed(range(count)) if reverse else range(count):
            passed = k > position if reverse else k < position
            total = combine(total, jax.tree.map(lambda part: part[k], pieces))
            inside = jax.tree.map(lambda new, old: jnp.where(passed, new, old), total, inside)
        before = combine(inside, before)
    return before


def over_axes(value, axes):
    return functools.reduce(lax.psum, axes, value)


def decay_logs(decay_index, table_len, seq_len):
    table_pos = jnp.arange(table_len, dtype=jnp.float32)
    fast_log = jnp.log(jnp.float32(1.0 / 32.0))
    slow_log = jnp.log(jnp.float32(1.0 / (64.0 * seq_len)))
    table_rates = jnp.exp(fast_log + table_pos / (table_len - 1) * (slow_log - fast_log))
    matches = decay_index[:, None] == jnp.arange(table_len, dtype=jnp.int32)[None, :]
    picked = jnp.sum(jnp.where(matches, table_rates[None, :], 0.0), axis=1)
    return -picked


def block_factors(log_decay, reset_block):
    block_len = reset_block.shape[0]
    segment_ids = jnp.cumsum(reset_block)
    places = jnp.arange(block_len, dtype=jnp.float32)
    causal = places[:, None] >= places[None, :]
    joined = segment_ids[:, None] == segment_ids[None, :]
    allowed = jnp.logical_and(causal, joined)[None, :, :]
    exponents = (places[:, None] - places[None, :])[None, :, :] * log_decay[:, None, None]
    within = jnp.where(allowed, jnp.exp(jnp.where(allowed, exponents, 0.0)), 0.0)
    first_seg = (segment_ids == 0).astype(jnp.float32)
    last_seg = (segment_ids == segment_ids[-1]).astype(jnp.float32)
    opening = jnp.exp((places + 1.0)[None, :] * log_decay[:, None]) * first_seg[None, :]
    closing = jnp.exp((block_len - 1.0 - places)[None, :] * log_decay[:, None]) * last_seg[None, :]
    carry_decay = jnp.exp(block_len * log_decay) * (segment_ids[-1] == 0).astype(jnp.float32)
    return (within, opening, closing, carry_decay)


def forward_local(query3, key3, value3, within, closing):
    scores = jnp.einsum("thd,shd->hts", query3, key3, preferred_element_type=jnp.float32)
    weights = (within * scores).astype(jnp.bfloat16)
    weighted = key3.astype(jnp.float32) * jnp.transpose(closing)[:, :, None]
    local_state = jnp.einsum(
        "thd,the->hde", weighted, value3.astype(jnp.float32), precision=highest
    )
    return (weights, local_state)


def forward_output(weights, query3, value3, opening, state_in):
    inner = jnp.einsum("hts,she->the", weights, value3, preferred_element_type=jnp.float32)
    reached = query3.astype(jnp.float32) * jnp.transpose(opening)[:, :, None]
    return inner + jnp.einsum("thd,hde->the", reached, state_in, precision=highest)


def head_norm(attended):
    inv_rms = lax.rsqrt(jnp.mean(attended * attended, axis=-1, keepdims=True) + norm_eps)
    return (attended * inv_rms, inv_rms)


def backward_norm(normed, inv_rms, grad_normed):
    product_mean = jnp.mean(grad_normed * normed, axis=-1, keepdims=True)
    return (inv_rms * (grad_normed - normed * product_mean)).astype(jnp.bfloat16)


def grad_state(query3, grad3, opening):
    reached = query3.astype(jnp.float32) * jnp.transpose(opening)[:, :, None]
    return jnp.einsum("thd,the->hde", reached, grad3.astype(jnp.float32), precision=highest)


def backward_block(
    weights, within, opening, closing, query3, key3, value3, grad3, state_in, state_after
):
    open_t = jnp.transpose(opening)[:, :, None]
    close_t = jnp.transpose(closing)[:, :, None]
    mixing = (
        within * jnp.einsum("the,she->hts", grad3, value3, preferred_element_type=jnp.float32)
    ).astype(jnp.bfloat16)
    grad_query = jnp.einsum(
        "hts,shd->thd", mixing, key3, preferred_element_type=jnp.float32
    ) + jnp.einsum("the,hde->thd", grad3.astype(jnp.float32) * open_t, state_in, precision=highest)
    grad_key = jnp.einsum(
        "hts,thd->shd", mixing, query3, preferred_element_type=jnp.float32
    ) + jnp.einsum(
        "the,hde->thd", value3.astype(jnp.float32) * close_t, state_after, precision=highest
    )
    grad_value = jnp.einsum(
        "hts,the->she", weights, grad3, preferred_element_type=jnp.float32
    ) + jnp.einsum(
        "thd,hde->the", key3.astype(jnp.float32) * close_t, state_after, precision=highest
    )
    return (
        grad_query.astype(jnp.bfloat16),
        grad_key.astype(jnp.bfloat16),
        grad_value.astype(jnp.bfloat16),
    )


def chain_blocks(earlier, succeeding):
    return (earlier[0] * succeeding[0], succeeding[0][:, None, None] * earlier[1] + succeeding[1])


def local(
    hidden, w_gate, query_rows, key_rows, value_rows, target, decay_index, loss_mask, doc_reset
):
    tokens_dev = hidden.shape[1]
    heads_dev = decay_index.shape[0]
    head_size = query_rows.shape[2] // heads_dev
    seq_count = lax.axis_size(SEQ)
    log_decay = decay_logs(decay_index, TABLE, tokens_dev * seq_count)
    mask_rows = loss_mask[0].astype(jnp.float32)
    count_dev = jnp.sum(mask_rows)
    columns = hidden[0]
    gate_pre = jnp.dot(
        columns,
        lax.all_gather(w_gate, "dp", axis=0, tiled=True),
        preferred_element_type=jnp.float32,
    )
    gate_val = jax.nn.sigmoid(gate_pre).reshape(tokens_dev, heads_dev, head_size)
    query3 = query_rows[0].reshape(tokens_dev, heads_dev, head_size)
    key3 = key_rows[0].reshape(tokens_dev, heads_dev, head_size)
    value3 = value_rows[0].reshape(tokens_dev, heads_dev, head_size)
    target3 = target[0].reshape(tokens_dev, heads_dev, head_size)
    within, opening, closing, carry_decay = block_factors(log_decay, doc_reset[0])
    weights, local_state = forward_local(query3, key3, value3, within, closing)
    identity = (
        jnp.ones((heads_dev,), jnp.float32),
        jnp.zeros((heads_dev, head_size, head_size), jnp.float32),
    )
    state_in = entering((carry_decay, local_state), SEQ, chain_blocks, identity, False)[1]
    attended = forward_output(weights, query3, value3, opening, state_in)
    normed, inv_rms = head_norm(attended)
    gated = normed * gate_val
    errors = gated - target3.astype(jnp.float32)
    mask3 = mask_rows[:, None, None]
    square_sum = jnp.sum(mask3 * errors * errors)
    count_sum, error_all = (over_axes(count_dev, DP_SEQ_HEADS), over_axes(square_sum, DP_SEQ_HEADS))
    count_all = count_sum / lax.axis_size("heads")
    weight_total = lax.axis_size("dp") * seq_count * tokens_dev / count_all
    grad_gated = weight_total * mask3 * errors
    grad_gate = (grad_gated * normed * gate_val * (1.0 - gate_val)).astype(jnp.bfloat16)
    grad_out = backward_norm(normed, inv_rms, grad_gated * gate_val)
    local_grad = grad_state(query3, grad_out, opening)
    state_after = entering((carry_decay, local_grad), SEQ, chain_blocks, identity, True)[1]
    grad_query, grad_key, grad_value = backward_block(
        weights, within, opening, closing, query3, key3, value3, grad_out, state_in, state_after
    )
    mean_loss = error_all / (2.0 * count_all * (heads_dev * lax.axis_size("heads") * head_size))
    flat = (1, tokens_dev, heads_dev * head_size)
    return (
        gated.astype(jnp.bfloat16).reshape(flat),
        grad_gate.reshape(flat),
        grad_query.reshape(flat),
        grad_key.reshape(flat),
        grad_value.reshape(flat),
        mean_loss,
    )


def solution(mesh):
    finer = Mesh(
        mesh.devices.reshape(mesh.shape["dp"], 8, 2, mesh.shape["heads"]),
        ("dp", "seq_0", "seq_1", "heads"),
    )
    placed = (
        P("dp", SEQ, None),
        P("dp", "heads"),
        P("dp", SEQ, "heads"),
        P("dp", SEQ, "heads"),
        P("dp", SEQ, "heads"),
        P("dp", SEQ, "heads"),
        P("heads"),
        P("dp", SEQ),
        P("dp", SEQ),
    )
    return jax.shard_map(
        local,
        mesh=finer,
        in_specs=placed,
        out_specs=(
            P("dp", SEQ, "heads"),
            P("dp", SEQ, "heads"),
            P("dp", SEQ, "heads"),
            P("dp", SEQ, "heads"),
            P("dp", SEQ, "heads"),
            P(),
        ),
        check_vma=False,
    )
```

profile of v0, /device:TPU:2, one launch (start us, length us, event | category | flops | bytes accessed | tf_op | source)
XLA Modules:
  0.0 232.2 jit_solution(15989236934014904022)
XLA Ops:
  7.3 1.1 reduce-window.9
  10.6 1.3 dynamic-slice.1
  11.9 1.3 dynamic-slice
  14.5 0.8 fusion.68
  15.4 3.0 %all-reduce = f32[4]{0:T(128)} all-reduce(f32[4]{0:T(128)S(1)} %get-tuple-element.58), channel_id=2, replica_groups=mesh['dp'=4,'seq_0'=8,'seq_1'=2,'heads'=16] {'seq_1'}, use_global_device_ids=true, to_apply=%add | all-reduce | flops 4 | bytes 32
  18.4 0.9 reshape_squeeze.11
  19.3 1.0 reshape_squeeze.12
  21.5 2.0 all-gather.1
  24.0 1.4 broadcast_select_fusion.1
  25.9 0.7 bitcast_add_fusion.2
  26.7 0.7 all-gather.10.cloned.1.call-update
  27.5 1.3 convert_reduce_fusion
  28.7 21.5 %psum.56 = f32[]{:T(128)} all-reduce(f32[]{:T(128)} %convert_reduce_fusion), channel_id=1, replica_groups=mesh['dp'=4,'seq_0'=8,'seq_1'=2,'heads'=16] {'dp'}, use_global_device_ids=true, to_apply=%region_5.6 | all-reduce | flops 1 | bytes 8 | tf_op jit(solution)/shard_map/psum | solution.py:40
  50.2 14.8 %all-reduce.2 = (f32[16]{0:T(128)S(1)}, f32[]{:T(128)}) all-reduce(f32[16]{0:T(128)} %get-tuple-element.43, f32[]{:T(128)} %psum.56), channel_id=5, replica_groups=mesh['dp'=4,'seq_0'=8,'seq_1'=2,'heads'=16] {'seq_0'}, use_global_device_ids=true, to_apply=%add.1 | all-reduce | flops 17 | bytes 136
  65.1 3.1 %psum.58 = f32[]{:T(128)} all-reduce(f32[]{:T(128)} %get-tuple-element.33), channel_id=1, replica_groups=mesh['dp'=4,'seq_0'=8,'seq_1'=2,'heads'=16] {'seq_1'}, use_global_device_ids=true, to_apply=%region_7.8 | all-reduce | flops 1 | bytes 8 | tf_op jit(solution)/shard_map/psum | solution.py:40
  68.1 35.2 %psum.59 = f32[]{:T(128)} all-reduce(f32[]{:T(128)} %psum.58), channel_id=1, replica_groups=mesh['dp'=4,'seq_0'=8,'seq_1'=2,'heads'=16] {'heads'}, use_global_device_ids=true, to_apply=%region_8.9 | all-reduce | flops 1 | bytes 8 | tf_op jit(solution)/shard_map/psum | solution.py:40
  103.3 1.2 convert_element_type.86
  104.5 1.0 copy.81
  105.6 1.7 copy.90
  108.0 1.3 broadcast_multiply_fusion.1
  110.2 1.2 fusion.2
  112.1 1.9 convolution_bitcast_fusion.5
  114.0 1.6 fusion.44
  116.2 1.4 multiply_reduce_fusion.1
  117.6 14.3 %all-gather.10.cloned.1.call-done = bf16[6144,256]{1,0:T(8,128)(2,1)} async-done(((bf16[1536,256]{1,0:T(8,128)(2,1)}), bf16[6144,256]{1,0:T(8,128)(2,1)}) %all-gather.10.cloned.1.call-update) | async-done | bytes 3145744 | tf_op jit(solution)/shard_map/all_gather | solution.py:146
  131.9 3.3 %fusion.16 = f32[256,256]{0,1:T(8,128)S(1)} fusion(bf16[6144,256]{1,0:T(8,128)(2,1)} %all-gather.10.cloned.1.call-done, bf16[1,256,6144]{2,1,0:T(8,128)(2,1)S(1)} %copy-done), kind=kOutput, calls=%fused_computation.19 | convolution fusion | flops 805502976 | bytes 6553600 | tf_op jit(solution)/shard_map/dot_general | solution.py:144
  135.3 0.7 fusion.22
  136.0 0.8 multiply_convert_fusion
  137.7 2.0 all-gather.2
  139.7 0.7 bitcast_add_fusion
  140.5 9.7 %psum.60 = f32[]{:T(128)} all-reduce(f32[]{:T(128)} %get-tuple-element.30), channel_id=1, replica_groups=mesh['dp'=4,'seq_0'=8,'seq_1'=2,'heads'=16] {'dp'}, use_global_device_ids=true, to_apply=%region_11.12 | all-reduce | flops 1 | bytes 8 | tf_op jit(solution)/shard_map/psum | solution.py:40
  150.2 17.6 %psum.61 = f32[]{:T(128)} all-reduce(f32[]{:T(128)} %psum.60), channel_id=1, replica_groups=mesh['dp'=4,'seq_0'=8,'seq_1'=2,'heads'=16] {'seq_0'}, use_global_device_ids=true, to_apply=%region_12.13 | all-reduce | flops 1 | bytes 8 | tf_op jit(solution)/shard_map/psum | solution.py:40
  167.8 3.1 %psum.62 = f32[]{:T(128)} all-reduce(f32[]{:T(128)} %psum.61), channel_id=1, replica_groups=mesh['dp'=4,'seq_0'=8,'seq_1'=2,'heads'=16] {'seq_1'}, use_global_device_ids=true, to_apply=%region_13.14 | all-reduce | flops 1 | bytes 8 | tf_op jit(solution)/shard_map/psum | solution.py:40
  171.5 33.1 %psum.63 = f32[]{:T(128)} all-reduce(f32[]{:T(128)} %psum.62), channel_id=1, replica_groups=mesh['dp'=4,'seq_0'=8,'seq_1'=2,'heads'=16] {'heads'}, use_global_device_ids=true, to_apply=%region_14.15 | all-reduce | flops 1 | bytes 8 | tf_op jit(solution)/shard_map/psum | solution.py:40
  204.6 1.7 copy.99
  206.3 1.7 copy.98
  208.0 1.3 fusion.3
  209.3 0.7 copy-done.6
  210.0 1.1 convolution_bitcast_fusion.3
  211.2 2.0 fusion.19
  213.2 1.7 copy.100
  215.5 1.9 fusion.70
  217.4 1.5 fusion.33
  219.0 1.4 convolution_bitcast_fusion.1
  220.4 1.5 fusion.20
  221.9 1.1 fusion.21
  223.0 0.8 copy.101
  223.8 0.8 copy.102
  (63 shorter events, 7.2 us)
Async XLA Ops:
  7.2 124.8 %copy-start = (bf16[1,256,6144]{2,1,0:T(8,128)(2,1)S(1)}, bf16[1,256,6144]{2,1,0:T(8,128)(2,1)}, u32[]{:S(2)}) copy-start(bf16[1,256,6144]{2,1,0:T(8,128)(2,1)} %param.9) | copy-start | bytes 9437188
  7.2 106.8 %all-gather.8.cloned.1.call-start = ((), (), s32[]{:S(2)}) async-start(), calls=%async_computation | async-start | bytes 1179648 | tf_op jit(solution)/shard_map/all_gather | solution.py:29
  15.4 5.0 %copy-start.18 = (f32[2]{0:T(128)}, f32[2]{0:T(128)S(1)}, u32[]{:S(2)}) copy-start(f32[2]{0:T(128)S(1)} %get-tuple-element.59) | copy-start | bytes 28
  19.3 85.2 %copy-start.3 = (bf16[256,2,128]{2,1,0:T(2,128)(2,1)}, bf16[256,2,128]{2,1,0:T(2,128)(2,1)S(1)}, u32[]{:S(2)}) copy-start(bf16[256,2,128]{2,1,0:T(2,128)(2,1)S(1)} %reshape_squeeze.11) | copy-start | bytes 393220
  20.3 0.7 copy-start.4
  25.4 0.5 copy-start.17
  25.4 24.9 %copy-start.16 = (f32[2]{0:T(128)}, f32[2]{0:T(128)S(1)}, u32[]{:S(2)}) copy-start(f32[2]{0:T(128)S(1)} %get-tuple-element.40) | copy-start | bytes 28
  26.7 105.3 %all-gather.10.cloned.1.call-start = ((), (), s32[]{:S(2)}) async-start(), calls=%async_computation.1 | async-start | bytes 3932160 | tf_op jit(solution)/shard_map/all_gather | solution.py:146
  27.4 190.0 %all-gather.12.cloned.1.call-start = ((), (), s32[]{:S(2)}) async-start(), calls=%async_computation.2 | async-start | bytes 1179648 | tf_op jit(solution)/shard_map/all_gather | solution.py:29
  108.0 2.1 copy-start.8
  110.1 1.2 copy-start.9
  111.4 0.7 copy-start.7
  115.5 0.6 copy-start.5
  117.6 17.6 %copy-start.10 = (f32[1,256]{1,0:T(1,128)S(1)}, f32[1,256]{1,0:T(1,128)}, u32[]{:S(2)}) copy-start(f32[1,256]{1,0:T(1,128)} %convert_element_type.86) | copy-start | bytes 3076
  131.9 3.3 %copy-start.1 = (f32[1,256,256]{1,2,0:T(8,128)S(1)}, f32[1,256,256]{1,2,0:T(8,128)}, u32[]{:S(2)}) copy-start(f32[1,256,256]{1,2,0:T(8,128)} %copy.90) | copy-start | bytes 786436
  131.9 3.3 %copy-start.11 = (f32[256]{0:T(256)S(1)}, f32[256]{0:T(256)}, u32[]{:S(2)}) copy-start(f32[256]{0:T(256)} %broadcast_multiply_fusion.1) | copy-start | bytes 3076
  131.9 7.8 %copy-start.12 = (f32[2]{0:T(128)S(1)}, f32[2]{0:T(128)}, u32[]{:S(2)}) copy-start(f32[2]{0:T(128)} %get-tuple-element.41) | copy-start | bytes 28
  131.9 7.8 %copy-start.14 = (f32[2]{0:T(128)S(1)}, f32[2]{0:T(128)}, u32[]{:S(2)}) copy-start(f32[2]{0:T(128)} %get-tuple-element.45) | copy-start | bytes 28
  136.0 81.4 %copy-start.13 = (f32[2]{0:T(128)S(1)}, f32[2]{0:T(128)}, u32[]{:S(2)}) copy-start(f32[2]{0:T(128)} %get-tuple-element.41) | copy-start | bytes 28
  136.8 0.6 copy-start.2
  136.8 80.6 %copy-start.15 = (f32[2]{0:T(128)S(1)}, f32[2]{0:T(128)}, u32[]{:S(2)}) copy-start(f32[2]{0:T(128)} %get-tuple-element.45) | copy-start | bytes 28
  209.3 0.7 copy-start.6
Sparse Core Ops, SparseCore 0:
  26.8 53.6 all-gather.7
  83.2 48.6 all-gather.9
  140.6 47.1 all-gather.11
where the time goes:
time: 233 us; the launch traced here: 232 us
  blocking collectives  145 us (62%)
  between operations  19.1 us (8%)
  matrix products  19 us (8%)
  local copies, waits for them, and re-layouts  18.8 us (8%)
  other arithmetic  15.1 us (6%)
  waiting for transfers between devices  15 us (6%)
    psum x7, blocking collectives, over_axes(): return functools.reduce(lax.psum, axes, value)  123 us
    unnamed x2, blocking collectives  17.8 us
    unnamed x48, local copies, waits for them, and re-layouts  14.4 us
    all_gather x1, waiting for transfers between devices, local(): lax.all_gather(w_gate, 'dp', axis=0, tiled=True)  14.3 us
  transfers between devices with their start and end apart: 3, of which 1 were waited for; matrix products, arithmetic and copies ran while one was open for 11% of the time, Pallas kernels for 0%

commit v1 on v0

--- a/solution.py
+++ b/solution.py
@@ -1,5 +1,3 @@
-import functools
-
 import jax
 import jax.numpy as jnp
 from jax import lax
@@ -34,10 +32,6 @@
             inside = jax.tree.map(lambda new, old: jnp.where(passed, new, old), total, inside)
         before = combine(inside, before)
     return before
-
-
-def over_axes(value, axes):
-    return functools.reduce(lax.psum, axes, value)
 
 
 def decay_logs(decay_index, table_len, seq_len):
@@ -164,7 +158,8 @@
     errors = gated - target3.astype(jnp.float32)
     mask3 = mask_rows[:, None, None]
     square_sum = jnp.sum(mask3 * errors * errors)
-    count_sum, error_all = (over_axes(count_dev, DP_SEQ_HEADS), over_axes(square_sum, DP_SEQ_HEADS))
+    totals = lax.psum(jnp.stack([count_dev, square_sum]), DP_SEQ_HEADS)
+    count_sum, error_all = (totals[0], totals[1])
     count_all = count_sum / lax.axis_size("heads")
     weight_total = lax.axis_size("dp") * seq_count * tokens_dev / count_all
     grad_gated = weight_total * mask3 * errors

time: 233 us -> 326 us (1.40)
  the two profiles are of different devices: /device:TPU:2 before, /device:TPU:1 now
where the time goes in v1:
time: 326 us; the launch traced here: 321 us
  blocking collectives  155 us (48%)
  waiting for transfers between devices  89.9 us (28%)
  matrix products  19.8 us (6%)
  between operations  19.1 us (6%)
  local copies, waits for them, and re-layouts  18.5 us (6%)
  other arithmetic  17.8 us (5%)
    psum x1, blocking collectives, local(): totals = lax.psum(jnp.stack([count_dev, square_sum]), DP_SEQ_HEADS)  124 us
    all_gather x1, waiting for transfers between devices, local(): lax.all_gather(w_gate, 'dp', axis=0, tiled=True)  53.1 us
    all_gather x2, waiting for transfers between devices, entering(): pieces = jax.tree.map(lambda part: lax.all_gather(part, axis), total)  36.1 us
    unnamed x2, blocking collectives  27.1 us
    unnamed x46, local copies, waits for them, and re-layouts  13.4 us
  transfers between devices with their start and end apart: 3, of which 3 were waited for; matrix products, arithmetic and copies ran while one was open for 7% of the time, Pallas kernels for 0%

profile of v1, /device:TPU:1, one launch (start us, length us, event | category | flops | bytes accessed | tf_op | source)
XLA Modules:
  0.0 320.7 jit_solution(8112099180215590353)
XLA Ops:
  7.3 1.1 reduce-window.9
  10.6 1.3 dynamic-slice.1
  11.9 1.3 dynamic-slice
  14.5 0.8 fusion.70
  15.4 16.2 %all-reduce = f32[4]{0:T(128)S(1)} all-reduce(f32[4]{0:T(128)S(1)} %get-tuple-element.58), channel_id=2, replica_groups=mesh['dp'=4,'seq_0'=8,'seq_1'=2,'heads'=16] {'seq_1'}, use_global_device_ids=true, to_apply=%add | all-reduce | flops 4 | bytes 32
  31.6 0.9 reshape_squeeze.11
  32.6 1.0 reshape_squeeze.12
  34.7 2.0 all-gather.1
  37.4 0.7 bitcast_add_fusion.2
  38.2 0.7 all-gather.10.cloned.1.call-update
  39.0 1.2 convert_element_type.86
  40.3 1.0 copy.81
  41.3 1.8 copy.90
  43.1 10.9 %all-reduce.1 = f32[16]{0:T(128)S(1)} all-reduce(f32[16]{0:T(128)} %copy-done.17), channel_id=5, replica_groups=mesh['dp'=4,'seq_0'=8,'seq_1'=2,'heads'=16] {'seq_0'}, use_global_device_ids=true, to_apply=%add.1 | all-reduce | flops 16 | bytes 128
  54.0 1.3 convert_reduce_fusion
  55.3 0.7 fusion.73
  56.1 1.2 fusion.2
  57.4 0.7 copy-done.8
  58.1 1.9 convolution_bitcast_fusion.5
  60.0 14.4 %all-gather.8.cloned.1.call-done = f32[8,2,128,128]{3,2,1,0:T(8,128)} async-done(((f32[1,2,128,128]{3,2,1,0:T(8,128)}), f32[8,2,128,128]{3,2,1,0:T(8,128)}) %all-gather.8.cloned.1.call-update) | async-done | bytes 1048592 | tf_op jit(solution)/shard_map/all_gather | solution.py:27
  74.4 1.5 fusion.44
  76.6 1.4 multiply_reduce_fusion.1
  78.0 53.1 %all-gather.10.cloned.1.call-done = bf16[6144,256]{1,0:T(8,128)(2,1)} async-done(((bf16[1536,256]{1,0:T(8,128)(2,1)}), bf16[6144,256]{1,0:T(8,128)(2,1)}) %all-gather.10.cloned.1.call-update) | async-done | bytes 3145744 | tf_op jit(solution)/shard_map/all_gather | solution.py:140
  131.1 3.3 %fusion.16 = f32[256,256]{0,1:T(8,128)S(1)} fusion(bf16[6144,256]{1,0:T(8,128)(2,1)} %all-gather.10.cloned.1.call-done, bf16[1,256,6144]{2,1,0:T(8,128)(2,1)S(1)} %copy-done), kind=kOutput, calls=%fused_computation.19 | convolution fusion | flops 805502976 | bytes 6553600 | tf_op jit(solution)/shard_map/dot_general | solution.py:138
  134.4 0.7 copy-done.1
  135.1 1.4 fusion.22
  136.5 1.3 pad_maximum_fusion
  137.9 124.0 %psum.7 = f32[2]{0:T(128)S(1)} all-reduce(f32[2]{0:T(128)S(1)} %pad_maximum_fusion), channel_id=1, replica_groups=mesh['dp'=4,'seq_0'=8,'seq_1'=2,'heads'=16] {'dp','seq_0','seq_1','heads'}, use_global_device_ids=true, to_apply=%region_6.7 | all-reduce | flops 2 | bytes 16 | tf_op jit(solution)/shard_map/psum | solution.py:161
  263.1 1.1 multiply_reduce_fusion
  264.3 1.8 multiply_convert_fusion
  266.1 1.2 fusion.27
  267.2 2.3 all-gather.2
  269.6 1.4 bitcast_add_fusion
  271.0 1.7 copy.98
  273.3 1.7 copy.99
  275.0 1.3 fusion.3
  276.3 0.7 copy-done.7
  277.0 1.1 convolution_bitcast_fusion.3
  278.1 2.0 fusion.19
  280.1 1.7 copy.100
  282.3 1.9 fusion.74
  284.2 21.7 %all-gather.12.cloned.1.call-done = f32[8,2,128,128]{3,2,1,0:T(8,128)} async-done(((f32[1,2,128,128]{3,2,1,0:T(8,128)}), f32[8,2,128,128]{3,2,1,0:T(8,128)}) %all-gather.12.cloned.1.call-update) | async-done | bytes 1048592 | tf_op jit(solution)/shard_map/all_gather | solution.py:27
  305.8 1.5 fusion.33
  307.4 1.4 convolution_bitcast_fusion.1
  308.8 1.5 fusion.20
  310.3 1.2 fusion.21
  311.5 0.8 copy.101
  312.3 0.8 copy.102
  (58 shorter events, 5.1 us)
Async XLA Ops:
  7.2 124.0 %copy-start = (bf16[1,256,6144]{2,1,0:T(8,128)(2,1)S(1)}, bf16[1,256,6144]{2,1,0:T(8,128)(2,1)}, u32[]{:S(2)}) copy-start(bf16[1,256,6144]{2,1,0:T(8,128)(2,1)} %param.9) | copy-start | bytes 9437188
  7.2 67.2 %all-gather.8.cloned.1.call-start = ((), (), s32[]{:S(2)}) async-start(), calls=%async_computation | async-start | bytes 1179648 | tf_op jit(solution)/shard_map/all_gather | solution.py:27
  15.4 23.6 %copy-start.16 = (f32[2]{0:T(128)}, f32[2]{0:T(128)S(1)}, u32[]{:S(2)}) copy-start(f32[2]{0:T(128)S(1)} %get-tuple-element.59) | copy-start | bytes 28
  32.6 1.1 copy-start.3
  33.6 0.7 copy-start.4
  37.4 1.6 copy-start.15
  37.4 1.6 copy-start.17
  37.4 5.7 %copy-start.14 = (f32[2]{0:T(128)}, f32[2]{0:T(128)S(1)}, u32[]{:S(2)}) copy-start(f32[2]{0:T(128)S(1)} %get-tuple-element.40) | copy-start | bytes 28
  38.2 92.9 %all-gather.10.cloned.1.call-start = ((), (), s32[]{:S(2)}) async-start(), calls=%async_computation.1 | async-start | bytes 3932160 | tf_op jit(solution)/shard_map/all_gather | solution.py:140
  38.9 266.9 %all-gather.12.cloned.1.call-start = ((), (), s32[]{:S(2)}) async-start(), calls=%async_computation.2 | async-start | bytes 1179648 | tf_op jit(solution)/shard_map/all_gather | solution.py:27
  41.3 93.1 %copy-start.2 = (bf16[1,256,256]{1,2,0:T(8,128)(2,1)}, bf16[1,256,256]{1,2,0:T(8,128)(2,1)S(1)}, u32[]{:S(2)}) copy-start(bf16[1,256,256]{1,2,0:T(8,128)(2,1)S(1)} %copy.81) | copy-start | bytes 393220
  55.3 0.8 copy-start.9
  56.1 1.3 copy-start.10
  57.4 0.7 copy-start.8
  75.9 0.7 copy-start.5
  78.0 57.1 %copy-start.11 = (f32[1,256]{1,0:T(1,128)S(1)}, f32[1,256]{1,0:T(1,128)}, u32[]{:S(2)}) copy-start(f32[1,256]{1,0:T(1,128)} %convert_element_type.86) | copy-start | bytes 3076
  131.1 4.0 %copy-start.6 = (f32[1,256,256]{1,2,0:T(8,128)S(1)}, f32[1,256,256]{1,2,0:T(8,128)}, u32[]{:S(2)}) copy-start(f32[1,256,256]{1,2,0:T(8,128)} %copy.90) | copy-start | bytes 786436
  134.4 0.7 copy-start.1
  264.3 41.6 %copy-start.12 = (f32[2]{0:T(128)S(1)}, f32[2]{0:T(128)}, u32[]{:S(2)}) copy-start(f32[2]{0:T(128)} %get-tuple-element.41) | copy-start | bytes 28
  266.1 39.8 %copy-start.13 = (f32[2]{0:T(128)S(1)}, f32[2]{0:T(128)}, u32[]{:S(2)}) copy-start(f32[2]{0:T(128)} %get-tuple-element.45) | copy-start | bytes 28
  276.3 0.7 copy-start.7
Sparse Core Ops, SparseCore 0:
  38.3 36.0 all-gather.7
  77.1 54.0 all-gather.9
  271.1 34.6 all-gather.11

commit v2 on v1

v2 whole, which is shorter than its diff:
```python
import functools

import jax
import jax.numpy as jnp
import numpy as np
from jax import lax
from jax.experimental import pallas as pl
from jax.experimental.pallas import tpu as pltpu
from jax.sharding import PartitionSpec as P

TABLE = 16
NORM_EPS = 1e-06
CHUNKS = 4
F32, BF16 = jnp.float32, jnp.bfloat16
NN, NT, TN = ((1,), (0,)), ((1,), (1,)), ((0,), (0,))


def mm(a, b, dims=NN):
    return lax.dot_general(a, b, (dims, ((), ())), preferred_element_type=F32)


def split(x):
    hi = x.astype(BF16)
    return hi, (x - hi.astype(F32)).astype(BF16)


def farthest_first(n):
    return sorted(range(1, n), key=lambda d: -min(d, n - d))


def exchange(src, dst, axis, n, me, send, recv):
    copies = []
    for d in farthest_first(n):
        peer = lax.rem(me + d, n)
        copies.append(
            pltpu.make_async_remote_copy(
                src_ref=src(peer),
                dst_ref=dst(me),
                send_sem=send.at[d],
                recv_sem=recv.at[d],
                device_id={axis: peer},
                device_id_type=pl.DeviceIdType.MESH,
            )
        )
    return copies


def start(copies):
    for copy in copies:
        copy.start()


def arrived(copies):
    for copy in copies:
        copy.wait_recv()


def sent(copies):
    for copy in copies:
        copy.wait_send()


def kernel(
    n_dp, n_seq, n_heads,
    idx, mask_hbm, reset_hbm, hid_hbm, w_hbm, q_hbm, k_hbm, v_hbm, t_hbm,
    gated_ref, ggate_ref, gq_ref, gk_ref, gv_ref, loss_ref,
    hid, wbuf, qb, kb, vb, tb, mk, rs, gate_acc,
    within, pbuf, opening, closing, inner, gout, gkp, gvp,
    info, cnt, l1, l2, l3, s1src, s1, s2src, s2, g1src, g1, g2src, g2,
    loc, w_send, w_recv, sib_send, sib_recv, seq_send, seq_recv, dp_send, dp_recv, z_send, z_recv,
):
    x, b, z = lax.axis_index("dp"), lax.axis_index("seq"), lax.axis_index("heads")
    T = qb.shape[0]
    hd = gout.shape[2]
    heads_dev = gout.shape[0]
    depth = w_hbm.shape[0]
    piece = depth // 2 // CHUNKS
    rows = hd // n_seq
    core = lax.rem(b, 2)
    sibling = b + 1 - 2 * core
    ahead = lax.rem(x + 1 + 2 * core, n_dp)
    back = lax.rem(x + 3 - 2 * core, n_dp)
    across = lax.rem(x + 2, n_dp)

    barrier = pltpu.get_barrier_semaphore()
    for axis, n, me in (("seq", n_seq, b), ("dp", n_dp, x), ("heads", n_heads, z)):
        for d in farthest_first(n):
            pl.semaphore_signal(
                barrier, inc=1, device_id={axis: lax.rem(me + d, n)}, device_id_type=pl.DeviceIdType.MESH
            )
    local = [
        pltpu.make_async_copy(s, d, loc.at[i])
        for i, (s, d) in enumerate((
            (reset_hbm, rs), (mask_hbm, mk), (k_hbm.at[0], kb), (v_hbm.at[0], vb), (q_hbm.at[0], qb),
            (w_hbm, wbuf.at[x]), (hid_hbm.at[0], hid), (t_hbm.at[0], tb),
        ))
    ]
    start(local)

    local[0].wait()
    local[1].wait()
    row_i = lax.broadcasted_iota(jnp.int32, (T, T), 0)
    col_i = lax.broadcasted_iota(jnp.int32, (T, T), 1)
    lower = (col_i <= row_i).astype(F32).astype(BF16)
    upper = (row_i <= col_i).astype(F32).astype(BF16)
    flags = jnp.broadcast_to(rs[...].astype(F32), (T, T)).astype(BF16)
    seg_col = mm(lower, flags, NT)
    seg_row = mm(flags, upper)
    last = seg_col[T - 1:T, :hd]
    allowed = jnp.logical_and(col_i <= row_i, seg_col == seg_row)
    masks = jnp.broadcast_to(mk[...].astype(F32), (hd, T)).astype(BF16)
    mask_col = mm((col_i == row_i).astype(F32).astype(BF16), masks, NT)
    count_dev = mm(masks[:8], jnp.ones((T, hd), BF16))
    gap = (row_i - col_i).astype(F32)
    place = row_i[:, :hd].astype(F32)
    fast = float(np.log(np.float32(1.0 / 32.0)))
    slow = float(np.log(np.float32(1.0 / (64.0 * T * n_seq))))
    carries = []
    for h in range(heads_dev):
        entry = jnp.full((1, T), idx[h].astype(F32), F32)
        ell = -jnp.exp(fast + entry / (TABLE - 1) * (slow - fast))
        within[h] = jnp.where(allowed, jnp.exp(gap * ell), 0.0)
        ell = ell[:, :hd]
        opening[h] = jnp.where(seg_col[:, :hd] == 0.0, jnp.exp((place + 1.0) * ell), 0.0)
        closing[h] = jnp.where(seg_col[:, :hd] == last, jnp.exp((T - 1.0 - place) * ell), 0.0)
        carries.append(jnp.exp(T * ell))
    tile_row = lax.broadcasted_iota(jnp.int32, (8, hd), 0)
    info[b] = jnp.where(tile_row < 4, jnp.broadcast_to((last == 0.0).astype(F32), (8, hd)), count_dev)

    def head(ref, h):
        return ref[:, h * hd:(h + 1) * hd]

    local[2].wait()
    local[3].wait()
    for h in range(heads_dev):
        hi, lo = split(head(kb, h).astype(F32) * closing[h])
        value = head(vb, h)
        s1src[:, h] = (mm(hi, value, TN) + mm(lo, value, TN)).reshape(n_seq, rows, hd)

    pl.semaphore_wait(barrier, n_seq + n_dp + n_heads - 3)

    def w_piece(shard, half, i):
        return wbuf.at[shard, pl.ds(pl.multiple_of(half * (depth // 2) + i * piece, piece), piece), :]

    def w_copy(src, shard, i, route, peer):
        return pltpu.make_async_remote_copy(
            src_ref=src, dst_ref=w_piece(shard, core, i), send_sem=w_send.at[route, i], recv_sem=w_recv.at[route, i],
            device_id={"dp": peer}, device_id_type=pl.DeviceIdType.MESH,
        )

    def w_own(i):
        return w_hbm.at[pl.ds(pl.multiple_of(core * (depth // 2) + i * piece, piece), piece), :]

    def w_pass(shard, i, route):
        return pltpu.make_async_remote_copy(
            src_ref=w_piece(shard, core, i), dst_ref=w_piece(shard, core, i),
            send_sem=sib_send.at[route, i], recv_sem=sib_recv.at[route, i],
            device_id={"seq": sibling}, device_id_type=pl.DeviceIdType.MESH,
        )

    steps = range(CHUNKS)
    to_ahead = [w_copy(w_own(i), x, i, 0, ahead) for i in steps]
    to_back = [w_copy(w_own(i), x, i, 1, back) for i in steps]
    onward = [w_copy(w_piece(back, core, i), back, i, 2, ahead) for i in steps]
    passes = [[w_pass(shard, i, r) for i in steps] for r, shard in enumerate((back, ahead, across))]

    infos = exchange(lambda p: info.at[b], lambda me: info.at[me], "seq", n_seq, b, seq_send.at[0], seq_recv.at[0])
    states = exchange(lambda p: s1src.at[p], lambda me: s1.at[me], "seq", n_seq, b, seq_send.at[1], seq_recv.at[1])
    start(infos)
    start(states)
    for i in steps:
        to_ahead[i].start()
        to_back[i].start()
    s1[b] = s1src[b]

    local[4].wait()
    for h in range(heads_dev):
        scores = mm(head(qb, h), head(kb, h), NT)
        pbuf[h] = (within[h] * scores).astype(BF16)
        inner[h] = mm(pbuf[h], head(vb, h))

    def w_step(i):
        to_ahead[i].wait_recv()
        onward[i].start()
        passes[0][i].start()
        to_back[i].wait_recv()
        passes[1][i].start()

    def gate_part(shard, first=False):
        columns = pl.ds(pl.multiple_of(shard * depth, depth), depth)
        part = mm(hid[:, columns], wbuf[shard])
        gate_acc[...] = part if first else gate_acc[...] + part

    local[5].wait()
    local[6].wait()
    gate_part(x, first=True)
    w_step(0)
    arrived(infos)
    keep = [info[j, 0:1] for j in range(n_seq)]
    cnt[x] = functools.reduce(jnp.add, [info[j, 4:8] for j in range(n_seq)])
    counts = exchange(lambda p: cnt.at[x], lambda me: cnt.at[me], "dp", n_dp, x, dp_send.at[0], dp_recv.at[0])
    start(counts)

    def scan(source, result, order):
        for h in range(heads_dev):
            state = jnp.zeros((rows, hd), F32)
            for j in order:
                result[j, h] = state
                state = carries[h] * keep[j] * state + source[j, h]

    arrived(states)
    scan(s1, s2src, range(n_seq))
    states_in = exchange(lambda p: s2src.at[p], lambda me: s2.at[me], "seq", n_seq, b, seq_send.at[2], seq_recv.at[2])
    start(states_in)
    s2[b] = s2src[b]
    for i in steps[1:]:
        w_step(i)
    local[7].wait()
    arrived(states_in)
    state_in = [split(s2[:, h].reshape(hd, hd)) for h in range(heads_dev)]
    for h in range(heads_dev):
        query = head(qb, h)
        inner[h] = inner[h] + opening[h] * (mm(query, state_in[h][0]) + mm(query, state_in[h][1]))
    arrived(passes[1])
    gate_part(back)
    arrived(passes[0])
    gate_part(ahead)
    for i in steps:
        onward[i].wait_recv()
        passes[2][i].start()
    arrived(passes[2])
    gate_part(across)
    arrived(counts)
    count = functools.reduce(jnp.add, [cnt[j] for j in range(n_dp)])[0:1]
    scale = n_dp * n_seq * T / count

    square = jnp.zeros((8, hd), F32)
    for h in range(heads_dev):
        attended = inner[h]
        inv = lax.rsqrt(jnp.mean(attended * attended, axis=-1, keepdims=True) + NORM_EPS)
        normed = attended * inv
        gate = jax.nn.sigmoid(gate_acc[:, h * hd:(h + 1) * hd])
        gated = normed * gate
        errors = gated - head(tb, h).astype(F32)
        masked = mask_col * errors
        square = square + jnp.sum((masked * errors).reshape(T // 8, 8, hd), axis=0)
        grad_gated = scale * masked
        dn = grad_gated * gate
        gated_ref[0, :, h * hd:(h + 1) * hd] = gated.astype(BF16)
        ggate_ref[0, :, h * hd:(h + 1) * hd] = (dn * normed * (1.0 - gate)).astype(BF16)
        product = jnp.mean(dn * normed, axis=-1, keepdims=True)
        gout[h] = (inv * (dn - normed * product)).astype(BF16)
    l1[b] = square
    losses = exchange(lambda p: l1.at[b], lambda me: l1.at[me], "seq", n_seq, b, seq_send.at[3], seq_recv.at[3])
    start(losses)
    for h in range(heads_dev):
        hi, lo = split(head(qb, h).astype(F32) * opening[h])
        g1src[:, h] = (mm(hi, gout[h], TN) + mm(lo, gout[h], TN)).reshape(n_seq, rows, hd)
    grads = exchange(lambda p: g1src.at[p], lambda me: g1.at[me], "seq", n_seq, b, seq_send.at[4], seq_recv.at[4])
    start(grads)
    g1[b] = g1src[b]
    for h in range(heads_dev):
        grad = gout[h]
        mixing = (within[h] * mm(grad, head(vb, h), NT)).astype(BF16)
        carried = mm(grad, state_in[h][0], NT) + mm(grad, state_in[h][1], NT)
        gq_ref[0, :, h * hd:(h + 1) * hd] = (mm(mixing, head(kb, h)) + opening[h] * carried).astype(BF16)
        gkp[h] = mm(mixing, head(qb, h), TN)
        gvp[h] = mm(pbuf[h], grad, TN)
    arrived(losses)
    l2[x] = functools.reduce(jnp.add, [l1[j] for j in range(n_seq)])
    losses_dp = exchange(lambda p: l2.at[x], lambda me: l2.at[me], "dp", n_dp, x, dp_send.at[1], dp_recv.at[1])
    start(losses_dp)
    arrived(grads)
    scan(g1, g2src, range(n_seq - 1, -1, -1))
    states_after = exchange(lambda p: g2src.at[p], lambda me: g2.at[me], "seq", n_seq, b, seq_send.at[5], seq_recv.at[5])
    start(states_after)
    g2[b] = g2src[b]
    arrived(losses_dp)
    l3[z] = functools.reduce(jnp.add, [l2[j] for j in range(n_dp)])
    losses_z = exchange(lambda p: l3.at[z], lambda me: l3.at[me], "heads", n_heads, z, z_send, z_recv)
    start(losses_z)
    arrived(states_after)
    for h in range(heads_dev):
        hi, lo = split(g2[:, h].reshape(hd, hd))
        value, key = head(vb, h), head(kb, h)
        gk_ref[0, :, h * hd:(h + 1) * hd] = (gkp[h] + closing[h] * (mm(value, hi, NT) + mm(value, lo, NT))).astype(BF16)
        gv_ref[0, :, h * hd:(h + 1) * hd] = (gvp[h] + closing[h] * (mm(key, hi) + mm(key, lo))).astype(BF16)
    arrived(losses_z)
    total = functools.reduce(jnp.add, [l3[j] for j in range(n_heads)])
    loss_ref[0, 0] = jnp.sum(total / (2.0 * count * (heads_dev * n_heads * hd)))

    for copies in (to_ahead, to_back, onward, *passes, infos, states, counts, states_in, losses, grads, losses_dp, states_after, losses_z):
        sent(copies)


def local_step(sizes, hidden, w_gate, query_rows, key_rows, value_rows, target, decay_index, loss_mask, doc_reset):
    n_dp, n_seq, n_heads = sizes
    T, D = hidden.shape[1:]
    depth, width = w_gate.shape
    heads_dev = decay_index.shape[0]
    hd = width // heads_dev
    rows = hd // n_seq
    any_spec = pl.BlockSpec(memory_space=pl.ANY)
    out = jax.ShapeDtypeStruct((1, T, width), BF16)
    state = pltpu.VMEM((n_seq, heads_dev, rows, hd), F32)
    scratch = [
        pltpu.VMEM((T, D), BF16), pltpu.VMEM((n_dp, depth, width), BF16),
        *[pltpu.VMEM((T, width), BF16)] * 4,
        pltpu.VMEM((1, T), jnp.int32), pltpu.VMEM((1, T), jnp.int32), pltpu.VMEM((T, width), F32),
        pltpu.VMEM((heads_dev, T, T), F32), pltpu.VMEM((heads_dev, T, T), BF16),
        pltpu.VMEM((heads_dev, T, hd), F32), pltpu.VMEM((heads_dev, T, hd), F32), pltpu.VMEM((heads_dev, T, hd), F32),
        pltpu.VMEM((heads_dev, T, hd), BF16), pltpu.VMEM((heads_dev, T, hd), F32), pltpu.VMEM((heads_dev, T, hd), F32),
        pltpu.VMEM((n_seq, 8, hd), F32), pltpu.VMEM((n_dp, 4, hd), F32),
        pltpu.VMEM((n_seq, 8, hd), F32), pltpu.VMEM((n_dp, 8, hd), F32), pltpu.VMEM((n_heads, 8, hd), F32),
        *[state] * 8,
        pltpu.SemaphoreType.DMA((8,)),
        pltpu.SemaphoreType.DMA((3, CHUNKS)), pltpu.SemaphoreType.DMA((3, CHUNKS)),
        pltpu.SemaphoreType.DMA((3, CHUNKS)), pltpu.SemaphoreType.DMA((3, CHUNKS)),
        pltpu.SemaphoreType.DMA((6, n_seq)), pltpu.SemaphoreType.DMA((6, n_seq)),
        pltpu.SemaphoreType.DMA((2, n_dp)), pltpu.SemaphoreType.DMA((2, n_dp)),
        pltpu.SemaphoreType.DMA((n_heads,)), pltpu.SemaphoreType.DMA((n_heads,)),
    ]
    vmem, smem = pl.BlockSpec(memory_space=pltpu.VMEM), pl.BlockSpec(memory_space=pltpu.SMEM)
    *results, loss = pl.pallas_call(
        functools.partial(kernel, n_dp, n_seq, n_heads),
        out_shape=[out] * 5 + [jax.ShapeDtypeStruct((1, 1), F32)],
        in_specs=[smem] + [any_spec] * 8,
        out_specs=[vmem] * 5 + [smem],
        scratch_shapes=scratch,
        compiler_params=pltpu.CompilerParams(collective_id=0, has_side_effects=True),
        name="layer",
    )(decay_index, loss_mask, doc_reset, hidden, w_gate, query_rows, key_rows, value_rows, target)
    return (*results, loss.reshape(()))


def solution(mesh):
    sizes = tuple(mesh.shape[a] for a in ("dp", "seq", "heads"))
    rows = P("dp", "seq", "heads")
    return jax.shard_map(
        functools.partial(local_step, sizes),
        mesh=mesh,
        in_specs=(P("dp", "seq", None), P("dp", "heads"), rows, rows, rows, rows, P("heads"), P("dp", "seq"), P("dp", "seq")),
        out_specs=(rows, rows, rows, rows, rows, P()),
        check_vma=False,
    )
```

time: 326 us -> 70.3 us (0.22); the launches traced: 321 us -> 69.9 us
  blocking collectives: 155 us -> 0 us
  waiting for transfers between devices: 89.9 us -> 0 us
  Pallas kernels: 0 us -> 59.7 us
  matrix products: 19.8 us -> 0 us
  other arithmetic: 17.8 us -> 0 us
  between operations: 19.1 us -> 2.4 us
  local copies, waits for them, and re-layouts: 18.5 us -> 7.84 us
    psum x1 -> x0, blocking collectives: 124 us -> none  [local(): totals = lax.psum(jnp.stack([count_dev, square_sum]), DP_SEQ_HEADS)]
    all_gather x3 -> x0, waiting for transfers between devices: 89.2 us -> none  [the longest x1 53.1 us: local(): lax.all_gather(w_gate, 'dp', axis=0, tiled=True)]
    pallas_call x0 -> x1, Pallas kernels: none -> 59.7 us  [local_step(): pl.pallas_call(functools.partial(kernel, n_dp, n_seq, n_heads), out_shape...]
    unnamed x2 -> x0, blocking collectives: 27.1 us -> none
    dot_general x13 -> x0, matrix products: 19.8 us -> none  [the longest x1 3.28 us: local(): jnp.dot(columns, lax.all_gather(w_gate, 'dp', axis=0, tiled=True), prefer...]
    unnamed x46 -> x5, local copies, waits for them, and re-layouts: 13.4 us -> 7.84 us
    add x5 -> x0, other arithmetic: 5.21 us -> none  [the longest x4 5.2 us: chain_blocks(): succeeding[0][:, None, None] * earlier[1] + succeeding[1]]
    reduce_sum x4 -> x0, other arithmetic: 4.63 us -> none  [the longest x1 1.4 us: local(): square_sum = jnp.sum(mask3 * errors * errors)]
  transfers between devices with their start and end apart: 3 -> 0, of which waited for: 3 -> 0; matrix products, arithmetic and copies ran while one was open for 7% -> 0% of each run, Pallas kernels for 0% -> 0%
where the time goes in v2:
time: 70.3 us; the launch traced here: 69.9 us
  Pallas kernels  59.7 us (85%)
  local copies, waits for them, and re-layouts  7.84 us (11%)
  between operations  2.4 us (3%)
    pallas_call x1, Pallas kernels, local_step(): pl.pallas_call(functools.partial(kernel, n_dp, n_seq, n_heads), out_shape...  59.7 us
    unnamed x5, local copies, waits for them, and re-layouts  7.84 us

profile of v2, /device:TPU:1, one launch (start us, length us, event | category | flops | bytes accessed | tf_op | source)
XLA Modules:
  0.0 69.9 jit_solution(15631878599681129955)
XLA Ops:
  0.6 59.7 %layer.1 = (bf16[1,256,256]{2,1,0:T(8,128)(2,1)}, bf16[1,256,256]{2,1,0:T(8,128)(2,1)}, bf16[1,256,256]{2,1,0:T(8,128)(2,1)}, bf16[1,256,256]{2,1,0:T(8,128)(2,1...) custom-call(s32[2]{0:T(128)} %idx.1, s32[1,256]{1,0:T(1,128)} %mask_hbm.1, s32[1,256]{1,0:T(1,128)} %reset_hbm.1, ...), custom_call_target="tpu_custom_call" | custom-call | tf_op jit(solution)/shard_map/layer/pallas_call | solution.py:324
  60.3 1.6 %copy.21 = bf16[1,256,256]{2,1,0:T(8,128)(2,1)} copy(bf16[1,256,256]{2,1,0:T(8,128)(2,1)} %get-tuple-element.24) | data formatting | bytes 262144
  61.9 1.6 %copy.22 = bf16[1,256,256]{2,1,0:T(8,128)(2,1)} copy(bf16[1,256,256]{2,1,0:T(8,128)(2,1)} %get-tuple-element.25) | data formatting | bytes 262144
  63.4 1.6 %copy.23 = bf16[1,256,256]{2,1,0:T(8,128)(2,1)} copy(bf16[1,256,256]{2,1,0:T(8,128)(2,1)} %get-tuple-element.26) | data formatting | bytes 262144
  65.0 1.6 %copy.24 = bf16[1,256,256]{2,1,0:T(8,128)(2,1)} copy(bf16[1,256,256]{2,1,0:T(8,128)(2,1)} %get-tuple-element.27) | data formatting | bytes 262144
  66.6 1.6 %copy.25 = bf16[1,256,256]{2,1,0:T(8,128)(2,1)} copy(bf16[1,256,256]{2,1,0:T(8,128)(2,1)} %get-tuple-element.28) | data formatting | bytes 262144

commit v3 on v2

--- a/solution.py
+++ b/solution.py
@@ -11,6 +11,7 @@
 TABLE = 16
 NORM_EPS = 1e-06
 CHUNKS = 4
+STATE = jnp.bfloat16
 F32, BF16 = jnp.float32, jnp.bfloat16
 NN, NT, TN = ((1,), (0,)), ((1,), (1,)), ((0,), (0,))
 
@@ -45,6 +46,10 @@
     return copies
 
 
+def signal(sem, axis, peer):
+    pl.semaphore_signal(sem, inc=1, device_id={axis: peer}, device_id_type=pl.DeviceIdType.MESH)
+
+
 def start(copies):
     for copy in copies:
         copy.start()
@@ -64,10 +69,10 @@
     n_dp, n_seq, n_heads,
     idx, mask_hbm, reset_hbm, hid_hbm, w_hbm, q_hbm, k_hbm, v_hbm, t_hbm,
     gated_ref, ggate_ref, gq_ref, gk_ref, gv_ref, loss_ref,
-    hid, wbuf, qb, kb, vb, tb, mk, rs, gate_acc,
+    hid, wbuf, qb, kb, vb, tb, mk, rs, gate_acc, mask_col,
     within, pbuf, opening, closing, inner, gout, gkp, gvp,
     info, cnt, l1, l2, l3, s1src, s1, s2src, s2, g1src, g1, g2src, g2,
-    loc, w_send, w_recv, sib_send, sib_recv, seq_send, seq_recv, dp_send, dp_recv, z_send, z_recv,
+    loc, w_send, w_recv, sib_send, sib_recv, seq_send, seq_recv, dp_send, dp_recv, z_send, z_recv, ready,
 ):
     x, b, z = lax.axis_index("dp"), lax.axis_index("seq"), lax.axis_index("heads")
     T = qb.shape[0]
@@ -83,11 +88,10 @@
     across = lax.rem(x + 2, n_dp)
 
     barrier = pltpu.get_barrier_semaphore()
-    for axis, n, me in (("seq", n_seq, b), ("dp", n_dp, x), ("heads", n_heads, z)):
+    for axis, n, me, reach in (("seq", n_seq, b, n_seq), ("dp", n_dp, x, n_dp), ("heads", n_heads, z, 1)):
         for d in farthest_first(n):
-            pl.semaphore_signal(
-                barrier, inc=1, device_id={axis: lax.rem(me + d, n)}, device_id_type=pl.DeviceIdType.MESH
-            )
+            if min(d, n - d) <= reach:
+                signal(barrier, axis, lax.rem(me + d, n))
     local = [
         pltpu.make_async_copy(s, d, loc.at[i])
         for i, (s, d) in enumerate((
@@ -105,25 +109,20 @@
     upper = (row_i <= col_i).astype(F32).astype(BF16)
     flags = jnp.broadcast_to(rs[...].astype(F32), (T, T)).astype(BF16)
     seg_col = mm(lower, flags, NT)
-    seg_row = mm(flags, upper)
     last = seg_col[T - 1:T, :hd]
-    allowed = jnp.logical_and(col_i <= row_i, seg_col == seg_row)
     masks = jnp.broadcast_to(mk[...].astype(F32), (hd, T)).astype(BF16)
-    mask_col = mm((col_i == row_i).astype(F32).astype(BF16), masks, NT)
     count_dev = mm(masks[:8], jnp.ones((T, hd), BF16))
-    gap = (row_i - col_i).astype(F32)
     place = row_i[:, :hd].astype(F32)
     fast = float(np.log(np.float32(1.0 / 32.0)))
     slow = float(np.log(np.float32(1.0 / (64.0 * T * n_seq))))
-    carries = []
+    ells, carries = [], []
     for h in range(heads_dev):
         entry = jnp.full((1, T), idx[h].astype(F32), F32)
         ell = -jnp.exp(fast + entry / (TABLE - 1) * (slow - fast))
-        within[h] = jnp.where(allowed, jnp.exp(gap * ell), 0.0)
+        ells.append(ell)
         ell = ell[:, :hd]
-        opening[h] = jnp.where(seg_col[:, :hd] == 0.0, jnp.exp((place + 1.0) * ell), 0.0)
         closing[h] = jnp.where(seg_col[:, :hd] == last, jnp.exp((T - 1.0 - place) * ell), 0.0)
-        carries.append(jnp.exp(T * ell))
+        carries.append(jnp.broadcast_to(jnp.exp(T * ell), (rows, hd)))
     tile_row = lax.broadcasted_iota(jnp.int32, (8, hd), 0)
     info[b] = jnp.where(tile_row < 4, jnp.broadcast_to((last == 0.0).astype(F32), (8, hd)), count_dev)
 
@@ -132,12 +131,28 @@
 
     local[2].wait()
     local[3].wait()
-    for h in range(heads_dev):
-        hi, lo = split(head(kb, h).astype(F32) * closing[h])
-        value = head(vb, h)
-        s1src[:, h] = (mm(hi, value, TN) + mm(lo, value, TN)).reshape(n_seq, rows, hd)
-
-    pl.semaphore_wait(barrier, n_seq + n_dp + n_heads - 3)
+    def pack(ref, parts):
+        ref[...] = jnp.concatenate([p.reshape(n_seq, rows, hd) for p in parts], axis=1).astype(ref.dtype)
+
+    def unpack(ref, h):
+        state = ref[...].astype(F32)[:, h * rows:(h + 1) * rows].reshape(hd, hd)
+        return (state.astype(BF16),) if ref.dtype == BF16 else split(state)
+
+    def times(a, parts, dims=NN):
+        return functools.reduce(jnp.add, [mm(a, p, dims) for p in parts])
+
+    pack(s1src, [
+        functools.reduce(jnp.add, [mm(part, head(vb, h), TN) for part in split(head(kb, h).astype(F32) * closing[h])])
+        for h in range(heads_dev)
+    ])
+
+    pl.semaphore_wait(barrier, n_seq + n_dp)
+
+    def wave_signal(d, i):
+        for peer in (z + d, z + n_heads - d):
+            signal(ready.at[i], "heads", lax.rem(peer, n_heads))
+
+    wave_signal(1, 0)
 
     def w_piece(shard, half, i):
         return wbuf.at[shard, pl.ds(pl.multiple_of(half * (depth // 2) + i * piece, piece), piece), :]
@@ -174,7 +189,13 @@
     s1[b] = s1src[b]
 
     local[4].wait()
-    for h in range(heads_dev):
+    gap = (row_i - col_i).astype(F32)
+    seg_row = mm(flags, upper)
+    allowed = jnp.logical_and(col_i <= row_i, seg_col == seg_row)
+    mask_col[...] = mm((col_i == row_i).astype(F32).astype(BF16), masks, NT)
+    for h in range(heads_dev):
+        within[h] = jnp.where(allowed, jnp.exp(gap * ells[h]), 0.0)
+        opening[h] = jnp.where(seg_col[:, :hd] == 0.0, jnp.exp((place + 1.0) * ells[h][:, :hd]), 0.0)
         scores = mm(head(qb, h), head(kb, h), NT)
         pbuf[h] = (within[h] * scores).astype(BF16)
         inner[h] = mm(pbuf[h], head(vb, h))
@@ -195,18 +216,21 @@
     local[6].wait()
     gate_part(x, first=True)
     w_step(0)
+    pl.semaphore_wait(ready.at[0], 2)
+    wave_signal(2, 1)
     arrived(infos)
     keep = [info[j, 0:1] for j in range(n_seq)]
     cnt[x] = functools.reduce(jnp.add, [info[j, 4:8] for j in range(n_seq)])
     counts = exchange(lambda p: cnt.at[x], lambda me: cnt.at[me], "dp", n_dp, x, dp_send.at[0], dp_recv.at[0])
     start(counts)
 
+    carry = jnp.concatenate(carries, axis=0)
+
     def scan(source, result, order):
-        for h in range(heads_dev):
-            state = jnp.zeros((rows, hd), F32)
-            for j in order:
-                result[j, h] = state
-                state = carries[h] * keep[j] * state + source[j, h]
+        state = jnp.zeros((heads_dev * rows, hd), F32)
+        for j in order:
+            result[j] = state.astype(result.dtype)
+            state = carry * keep[j] * state + source[j].astype(F32)
 
     arrived(states)
     scan(s1, s2src, range(n_seq))
@@ -216,11 +240,12 @@
     for i in steps[1:]:
         w_step(i)
     local[7].wait()
+    pl.semaphore_wait(ready.at[1], 2)
+    wave_signal(4, 2)
     arrived(states_in)
-    state_in = [split(s2[:, h].reshape(hd, hd)) for h in range(heads_dev)]
-    for h in range(heads_dev):
-        query = head(qb, h)
-        inner[h] = inner[h] + opening[h] * (mm(query, state_in[h][0]) + mm(query, state_in[h][1]))
+    state_in = [unpack(s2, h) for h in range(heads_dev)]
+    for h in range(heads_dev):
+        inner[h] = inner[h] + opening[h] * times(head(qb, h), state_in[h])
     arrived(passes[1])
     gate_part(back)
     arrived(passes[0])
@@ -242,7 +267,7 @@
         gate = jax.nn.sigmoid(gate_acc[:, h * hd:(h + 1) * hd])
         gated = normed * gate
         errors = gated - head(tb, h).astype(F32)
-        masked = mask_col * errors
+        masked = mask_col[...] * errors
         square = square + jnp.sum((masked * errors).reshape(T // 8, 8, hd), axis=0)
         grad_gated = scale * masked
         dn = grad_gated * gate
@@ -253,16 +278,17 @@
     l1[b] = square
     losses = exchange(lambda p: l1.at[b], lambda me: l1.at[me], "seq", n_seq, b, seq_send.at[3], seq_recv.at[3])
     start(losses)
-    for h in range(heads_dev):
-        hi, lo = split(head(qb, h).astype(F32) * opening[h])
-        g1src[:, h] = (mm(hi, gout[h], TN) + mm(lo, gout[h], TN)).reshape(n_seq, rows, hd)
+    pack(g1src, [
+        functools.reduce(jnp.add, [mm(part, gout[h], TN) for part in split(head(qb, h).astype(F32) * opening[h])])
+        for h in range(heads_dev)
+    ])
     grads = exchange(lambda p: g1src.at[p], lambda me: g1.at[me], "seq", n_seq, b, seq_send.at[4], seq_recv.at[4])
     start(grads)
     g1[b] = g1src[b]
     for h in range(heads_dev):
         grad = gout[h]
         mixing = (within[h] * mm(grad, head(vb, h), NT)).astype(BF16)
-        carried = mm(grad, state_in[h][0], NT) + mm(grad, state_in[h][1], NT)
+        carried = times(grad, state_in[h], NT)
         gq_ref[0, :, h * hd:(h + 1) * hd] = (mm(mixing, head(kb, h)) + opening[h] * carried).astype(BF16)
         gkp[h] = mm(mixing, head(qb, h), TN)
         gvp[h] = mm(pbuf[h], grad, TN)
@@ -277,20 +303,28 @@
     g2[b] = g2src[b]
     arrived(losses_dp)
     l3[z] = functools.reduce(jnp.add, [l2[j] for j in range(n_dp)])
+    pl.semaphore_wait(ready.at[2], 2)
     losses_z = exchange(lambda p: l3.at[z], lambda me: l3.at[me], "heads", n_heads, z, z_send, z_recv)
     start(losses_z)
     arrived(states_after)
     for h in range(heads_dev):
-        hi, lo = split(g2[:, h].reshape(hd, hd))
-        value, key = head(vb, h), head(kb, h)
-        gk_ref[0, :, h * hd:(h + 1) * hd] = (gkp[h] + closing[h] * (mm(value, hi, NT) + mm(value, lo, NT))).astype(BF16)
-        gv_ref[0, :, h * hd:(h + 1) * hd] = (gvp[h] + closing[h] * (mm(key, hi) + mm(key, lo))).astype(BF16)
+        after = unpack(g2, h)
+        gk_ref[0, :, h * hd:(h + 1) * hd] = (gkp[h] + closing[h] * times(head(vb, h), after, NT)).astype(BF16)
+        gv_ref[0, :, h * hd:(h + 1) * hd] = (gvp[h] + closing[h] * times(head(kb, h), after)).astype(BF16)
     arrived(losses_z)
     total = functools.reduce(jnp.add, [l3[j] for j in range(n_heads)])
     loss_ref[0, 0] = jnp.sum(total / (2.0 * count * (heads_dev * n_heads * hd)))
 
     for copies in (to_ahead, to_back, onward, *passes, infos, states, counts, states_in, losses, grads, losses_dp, states_after, losses_z):
         sent(copies)
+
+
+def deliver(*refs):
+    *arrays, sems = refs
+    copies = [pltpu.make_async_copy(arrays[i], arrays[i + 5], sems.at[i]) for i in range(5)]
+    start(copies)
+    for copy in copies:
+        copy.wait()
 
 
 def local_step(sizes, hidden, w_gate, query_rows, key_rows, value_rows, target, decay_index, loss_mask, doc_reset):
@@ -302,11 +336,12 @@
     rows = hd // n_seq
     any_spec = pl.BlockSpec(memory_space=pl.ANY)
     out = jax.ShapeDtypeStruct((1, T, width), BF16)
-    state = pltpu.VMEM((n_seq, heads_dev, rows, hd), F32)
+    held = pltpu.VMEM((1, T, width), BF16)
+    state = pltpu.VMEM((n_seq, heads_dev * rows, hd), STATE)
     scratch = [
         pltpu.VMEM((T, D), BF16), pltpu.VMEM((n_dp, depth, width), BF16),
         *[pltpu.VMEM((T, width), BF16)] * 4,
-        pltpu.VMEM((1, T), jnp.int32), pltpu.VMEM((1, T), jnp.int32), pltpu.VMEM((T, width), F32),
+        pltpu.VMEM((1, T), jnp.int32), pltpu.VMEM((1, T), jnp.int32), pltpu.VMEM((T, width), F32), pltpu.VMEM((T, hd), F32),
         pltpu.VMEM((heads_dev, T, T), F32), pltpu.VMEM((heads_dev, T, T), BF16),
         pltpu.VMEM((heads_dev, T, hd), F32), pltpu.VMEM((heads_dev, T, hd), F32), pltpu.VMEM((heads_dev, T, hd), F32),
         pltpu.VMEM((heads_dev, T, hd), BF16), pltpu.VMEM((heads_dev, T, hd), F32), pltpu.VMEM((heads_dev, T, hd), F32),
@@ -318,18 +353,26 @@
         pltpu.SemaphoreType.DMA((3, CHUNKS)), pltpu.SemaphoreType.DMA((3, CHUNKS)),
         pltpu.SemaphoreType.DMA((6, n_seq)), pltpu.SemaphoreType.DMA((6, n_seq)),
         pltpu.SemaphoreType.DMA((2, n_dp)), pltpu.SemaphoreType.DMA((2, n_dp)),
-        pltpu.SemaphoreType.DMA((n_heads,)), pltpu.SemaphoreType.DMA((n_heads,)),
+        pltpu.SemaphoreType.DMA((n_heads,)), pltpu.SemaphoreType.DMA((n_heads,)), pltpu.SemaphoreType.REGULAR((3,)),
     ]
     vmem, smem = pl.BlockSpec(memory_space=pltpu.VMEM), pl.BlockSpec(memory_space=pltpu.SMEM)
     *results, loss = pl.pallas_call(
         functools.partial(kernel, n_dp, n_seq, n_heads),
-        out_shape=[out] * 5 + [jax.ShapeDtypeStruct((1, 1), F32)],
+        out_shape=[held] * 5 + [jax.ShapeDtypeStruct((1, 1), F32)],
         in_specs=[smem] + [any_spec] * 8,
         out_specs=[vmem] * 5 + [smem],
         scratch_shapes=scratch,
         compiler_params=pltpu.CompilerParams(collective_id=0, has_side_effects=True),
         name="layer",
     )(decay_index, loss_mask, doc_reset, hidden, w_gate, query_rows, key_rows, value_rows, target)
+    results = pl.pallas_call(
+        deliver,
+        out_shape=[out] * 5,
+        in_specs=[vmem] * 5,
+        out_specs=[any_spec] * 5,
+        scratch_shapes=[pltpu.SemaphoreType.DMA((5,))],
+        name="deliver",
+    )(*[pltpu.with_memory_space_constraint(r, pltpu.VMEM) for r in results])
     return (*results, loss.reshape(()))
 
 

time: 70.3 us -> 59.1 us (0.84)
  local copies, waits for them, and re-layouts: 7.84 us -> 0 us
  Pallas kernels: 59.7 us -> 56.5 us
    unnamed x5 -> x0, local copies, waits for them, and re-layouts: 7.84 us -> none
    pallas_call x1, Pallas kernels: 59.7 us -> 55.7 us  [local_step(): pl.pallas_call(functools.partial(kernel, n_dp, n_seq, n_heads), out_shape...]
    pallas_call x0 -> x1, Pallas kernels: none -> 0.87 us  [local_step(): pl.pallas_call(deliver, out_shape=[out] * 5, in_specs=[vmem] * 5, out_spe...]
where the time goes in v3:
time: 59.1 us; the launch traced here: 59 us
  Pallas kernels  56.5 us (96%)
  between operations  2.41 us (4%)
    pallas_call x1, Pallas kernels, local_step(): pl.pallas_call(functools.partial(kernel, n_dp, n_seq, n_heads), out_shape...  55.7 us

profile of v3, /device:TPU:1, one launch (start us, length us, event | category | flops | bytes accessed | tf_op | source)
XLA Modules:
  0.0 59.0 jit_solution(13581071748513265136)
XLA Ops:
  0.6 55.7 %layer.1 = (bf16[1,256,256]{2,1,0:T(8,128)(2,1)S(1)}, bf16[1,256,256]{2,1,0:T(8,128)(2,1)S(1)}, bf16[1,256,256]{2,1,0:T(8,128)(2,1)S(1)}, bf16[1,256,256]{2,1,0:...) custom-call(s32[2]{0:T(128)} %idx.1, s32[1,256]{1,0:T(1,128)} %mask_hbm.1, s32[1,256]{1,0:T(1,128)} %reset_hbm.1, ...), custom_call_target="tpu_custom_call" | custom-call | tf_op jit(solution)/shard_map/layer/pallas_call | solution.py:359
  56.3 0.9 %deliver.1 = (bf16[1,256,256]{2,1,0:T(8,128)(2,1)}, bf16[1,256,256]{2,1,0:T(8,128)(2,1)}, bf16[1,256,256]{2,1,0:T(8,128)(2,1)}, bf16[1,256,256]{2,1,0:T(8,128)(2,1)}, bf16[1,256,256]{2,1,0:T(8,128)(2,1)}) custom-call(bf16[1,256,256]{2,1,0:T(8,128)(2,1)S(1)} %get-tuple-element.17.refs_0_, bf16[1,256,256]{2,1,0:T(8,128)(2,1)S(1)} %get-tuple-element.18.refs_1_, ...), custom_call_target="tpu_custom_call" | custom-call | tf_op jit(solution)/shard_map/deliver/pallas_call | solution.py:368

commit v4 on v3

--- a/solution.py
+++ b/solution.py
@@ -10,7 +10,7 @@
 
 TABLE = 16
 NORM_EPS = 1e-06
-CHUNKS = 4
+CHUNKS = 3
 STATE = jnp.bfloat16
 F32, BF16 = jnp.float32, jnp.bfloat16
 NN, NT, TN = ((1,), (0,)), ((1,), (1,)), ((0,), (0,))
@@ -67,42 +67,48 @@
 
 def kernel(
     n_dp, n_seq, n_heads,
-    idx, mask_hbm, reset_hbm, hid_hbm, w_hbm, q_hbm, k_hbm, v_hbm, t_hbm,
+    idx_hbm, mask_hbm, reset_hbm, hid_hbm, w_hbm, q_hbm, k_hbm, v_hbm, t_hbm,
     gated_ref, ggate_ref, gq_ref, gk_ref, gv_ref, loss_ref,
-    hid, wbuf, qb, kb, vb, tb, mk, rs, gate_acc, mask_col,
+    idx, hid, wbuf, qb, kb, vb, tb, mk, rs, gate_acc, mask_col,
     within, pbuf, opening, closing, inner, gout, gkp, gvp,
     info, cnt, l1, l2, l3, s1src, s1, s2src, s2, g1src, g1, g2src, g2,
-    loc, w_send, w_recv, sib_send, sib_recv, seq_send, seq_recv, dp_send, dp_recv, z_send, z_recv, ready,
+    loc, w_send, w_recv, seq_send, seq_recv, dp_send, dp_recv, z_send, z_recv, ready,
 ):
     x, b, z = lax.axis_index("dp"), lax.axis_index("seq"), lax.axis_index("heads")
     T = qb.shape[0]
     hd = gout.shape[2]
     heads_dev = gout.shape[0]
     depth = w_hbm.shape[0]
-    piece = depth // 2 // CHUNKS
+    piece = depth // 4 // CHUNKS
     rows = hd // n_seq
     core = lax.rem(b, 2)
     sibling = b + 1 - 2 * core
     ahead = lax.rem(x + 1 + 2 * core, n_dp)
     back = lax.rem(x + 3 - 2 * core, n_dp)
     across = lax.rem(x + 2, n_dp)
-
+    row = b // 2
+    beside = 2 * lax.rem(row + n_seq // 2 - 1 + 2 * core, n_seq // 2) + core
+    quarter = 2 * lax.rem(row, 2) + core
+    other = 2 * (1 - lax.rem(row, 2)) + core
+
+    local = [
+        pltpu.make_async_copy(s, d, loc.at[i])
+        for i, (s, d) in enumerate((
+            (reset_hbm, rs), (idx_hbm, idx), (k_hbm.at[0], kb), (v_hbm.at[0], vb), (mask_hbm, mk), (q_hbm.at[0], qb),
+            (w_hbm, wbuf.at[x]), (hid_hbm.at[0], hid), (t_hbm.at[0], tb),
+        ))
+    ]
+    start(local[:5])
     barrier = pltpu.get_barrier_semaphore()
     for axis, n, me, reach in (("seq", n_seq, b, n_seq), ("dp", n_dp, x, n_dp), ("heads", n_heads, z, 1)):
         for d in farthest_first(n):
             if min(d, n - d) <= reach:
                 signal(barrier, axis, lax.rem(me + d, n))
-    local = [
-        pltpu.make_async_copy(s, d, loc.at[i])
-        for i, (s, d) in enumerate((
-            (reset_hbm, rs), (mask_hbm, mk), (k_hbm.at[0], kb), (v_hbm.at[0], vb), (q_hbm.at[0], qb),
-            (w_hbm, wbuf.at[x]), (hid_hbm.at[0], hid), (t_hbm.at[0], tb),
-        ))
-    ]
-    start(local)
+    start(local[5:])
 
     local[0].wait()
     local[1].wait()
+    local[4].wait()
     row_i = lax.broadcasted_iota(jnp.int32, (T, T), 0)
     col_i = lax.broadcasted_iota(jnp.int32, (T, T), 1)
     lower = (col_i <= row_i).astype(F32).astype(BF16)
@@ -123,8 +129,8 @@
         ell = ell[:, :hd]
         closing[h] = jnp.where(seg_col[:, :hd] == last, jnp.exp((T - 1.0 - place) * ell), 0.0)
         carries.append(jnp.broadcast_to(jnp.exp(T * ell), (rows, hd)))
-    tile_row = lax.broadcasted_iota(jnp.int32, (8, hd), 0)
-    info[b] = jnp.where(tile_row < 4, jnp.broadcast_to((last == 0.0).astype(F32), (8, hd)), count_dev)
+    info[b, 0:1] = (last == 0.0).astype(F32)
+    info[b, 1:2] = count_dev[0:1]
 
     def head(ref, h):
         return ref[:, h * hd:(h + 1) * hd]
@@ -154,41 +160,50 @@
 
     wave_signal(1, 0)
 
-    def w_piece(shard, half, i):
-        return wbuf.at[shard, pl.ds(pl.multiple_of(half * (depth // 2) + i * piece, piece), piece), :]
-
-    def w_copy(src, shard, i, route, peer):
+    def w_piece(shard, part, i):
+        return wbuf.at[shard, pl.ds(pl.multiple_of(part * (depth // 4) + i * piece, piece), piece), :]
+
+    def w_copy(kind, route, shard, part, i, target, src=None):
         return pltpu.make_async_remote_copy(
-            src_ref=src, dst_ref=w_piece(shard, core, i), send_sem=w_send.at[route, i], recv_sem=w_recv.at[route, i],
-            device_id={"dp": peer}, device_id_type=pl.DeviceIdType.MESH,
+            src_ref=w_piece(shard, part, i) if src is None else src, dst_ref=w_piece(shard, part, i),
+            send_sem=w_send.at[kind, route, i], recv_sem=w_recv.at[kind, route, i],
+            device_id=target, device_id_type=pl.DeviceIdType.MESH,
         )
 
-    def w_own(i):
-        return w_hbm.at[pl.ds(pl.multiple_of(core * (depth // 2) + i * piece, piece), piece), :]
-
-    def w_pass(shard, i, route):
-        return pltpu.make_async_remote_copy(
-            src_ref=w_piece(shard, core, i), dst_ref=w_piece(shard, core, i),
-            send_sem=sib_send.at[route, i], recv_sem=sib_recv.at[route, i],
-            device_id={"seq": sibling}, device_id_type=pl.DeviceIdType.MESH,
-        )
-
     steps = range(CHUNKS)
-    to_ahead = [w_copy(w_own(i), x, i, 0, ahead) for i in steps]
-    to_back = [w_copy(w_own(i), x, i, 1, back) for i in steps]
-    onward = [w_copy(w_piece(back, core, i), back, i, 2, ahead) for i in steps]
-    passes = [[w_pass(shard, i, r) for i in steps] for r, shard in enumerate((back, ahead, across))]
+    own = [w_hbm.at[pl.ds(pl.multiple_of(quarter * (depth // 4) + i * piece, piece), piece), :] for i in steps]
+    shards = (back, ahead, across)
+    ring = [
+        [w_copy(0, 0, x, quarter, i, {"dp": ahead}, own[i]) for i in steps],
+        [w_copy(0, 1, x, quarter, i, {"dp": back}, own[i]) for i in steps],
+        [w_copy(0, 2, back, quarter, i, {"dp": ahead}) for i in steps],
+    ]
+    share = [[w_copy(1, r, shards[r], quarter, i, {"seq": sibling}) for i in steps] for r in range(3)]
+    step_y = [[w_copy(2, r, shards[r], quarter, i, {"seq": beside}) for i in steps] for r in range(3)]
+    relay = [[w_copy(3, r, shards[r], other, i, {"seq": sibling}) for i in steps] for r in range(3)]
+
+    def from_ring(r, i):
+        ring[r][i].wait_recv()
+        if r == 0:
+            ring[2][i].start()
+        step_y[r][i].start()
+        share[r][i].start()
+
+    def from_side(r, i):
+        step_y[r][i].wait_recv()
+        relay[r][i].start()
 
     infos = exchange(lambda p: info.at[b], lambda me: info.at[me], "seq", n_seq, b, seq_send.at[0], seq_recv.at[0])
     states = exchange(lambda p: s1src.at[p], lambda me: s1.at[me], "seq", n_seq, b, seq_send.at[1], seq_recv.at[1])
-    start(infos)
     start(states)
     for i in steps:
-        to_ahead[i].start()
-        to_back[i].start()
+        ring[0][i].start()
+        ring[1][i].start()
+        if i == 0:
+            start(infos)
     s1[b] = s1src[b]
 
-    local[4].wait()
+    local[5].wait()
     gap = (row_i - col_i).astype(F32)
     seg_row = mm(flags, upper)
     allowed = jnp.logical_and(col_i <= row_i, seg_col == seg_row)
@@ -200,27 +215,21 @@
         pbuf[h] = (within[h] * scores).astype(BF16)
         inner[h] = mm(pbuf[h], head(vb, h))
 
-    def w_step(i):
-        to_ahead[i].wait_recv()
-        onward[i].start()
-        passes[0][i].start()
-        to_back[i].wait_recv()
-        passes[1][i].start()
-
     def gate_part(shard, first=False):
         columns = pl.ds(pl.multiple_of(shard * depth, depth), depth)
         part = mm(hid[:, columns], wbuf[shard])
         gate_acc[...] = part if first else gate_acc[...] + part
 
-    local[5].wait()
     local[6].wait()
+    local[7].wait()
     gate_part(x, first=True)
-    w_step(0)
+    from_ring(0, 0)
+    from_ring(1, 0)
     pl.semaphore_wait(ready.at[0], 2)
     wave_signal(2, 1)
     arrived(infos)
     keep = [info[j, 0:1] for j in range(n_seq)]
-    cnt[x] = functools.reduce(jnp.add, [info[j, 4:8] for j in range(n_seq)])
+    cnt[x] = functools.reduce(jnp.add, [info[j, 1:2] for j in range(n_seq)])
     counts = exchange(lambda p: cnt.at[x], lambda me: cnt.at[me], "dp", n_dp, x, dp_send.at[0], dp_recv.at[0])
     start(counts)
 
@@ -232,34 +241,42 @@
             result[j] = state.astype(result.dtype)
             state = carry * keep[j] * state + source[j].astype(F32)
 
+    for i in steps[1:-1]:
+        from_ring(0, i)
+        from_ring(1, i)
     arrived(states)
     scan(s1, s2src, range(n_seq))
     states_in = exchange(lambda p: s2src.at[p], lambda me: s2.at[me], "seq", n_seq, b, seq_send.at[2], seq_recv.at[2])
     start(states_in)
     s2[b] = s2src[b]
-    for i in steps[1:]:
-        w_step(i)
-    local[7].wait()
+    from_ring(0, CHUNKS - 1)
+    from_ring(1, CHUNKS - 1)
+    local[8].wait()
     pl.semaphore_wait(ready.at[1], 2)
     wave_signal(4, 2)
+    for i in steps:
+        from_side(0, i)
+        from_side(1, i)
+        from_ring(2, i)
+    for copies in (*share[:2], *relay[:2]):
+        arrived(copies)
+    gate_part(back)
+    gate_part(ahead)
+    for i in steps:
+        from_side(2, i)
     arrived(states_in)
     state_in = [unpack(s2, h) for h in range(heads_dev)]
     for h in range(heads_dev):
         inner[h] = inner[h] + opening[h] * times(head(qb, h), state_in[h])
-    arrived(passes[1])
-    gate_part(back)
-    arrived(passes[0])
-    gate_part(ahead)
-    for i in steps:
-        onward[i].wait_recv()
-        passes[2][i].start()
-    arrived(passes[2])
+    arrived(share[2])
+    arrived(relay[2])
     gate_part(across)
     arrived(counts)
-    count = functools.reduce(jnp.add, [cnt[j] for j in range(n_dp)])[0:1]
+    count = functools.reduce(jnp.add, [cnt[j] for j in range(n_dp)])
     scale = n_dp * n_seq * T / count
 
-    square = jnp.zeros((8, hd), F32)
+    square = jnp.zeros((1, hd), F32)
+    invs = []
     for h in range(heads_dev):
         attended = inner[h]
         inv = lax.rsqrt(jnp.mean(attended * attended, axis=-1, keepdims=True) + NORM_EPS)
@@ -267,17 +284,21 @@
         gate = jax.nn.sigmoid(gate_acc[:, h * hd:(h + 1) * hd])
         gated = normed * gate
         errors = gated - head(tb, h).astype(F32)
-        masked = mask_col[...] * errors
-        square = square + jnp.sum((masked * errors).reshape(T // 8, 8, hd), axis=0)
-        grad_gated = scale * masked
-        dn = grad_gated * gate
+        square = square + jnp.sum(mask_col[...] * errors * errors, axis=0, keepdims=True)
         gated_ref[0, :, h * hd:(h + 1) * hd] = gated.astype(BF16)
-        ggate_ref[0, :, h * hd:(h + 1) * hd] = (dn * normed * (1.0 - gate)).astype(BF16)
-        product = jnp.mean(dn * normed, axis=-1, keepdims=True)
-        gout[h] = (inv * (dn - normed * product)).astype(BF16)
+        inner[h] = normed
+        gate_acc[:, h * hd:(h + 1) * hd] = gate
+        invs.append(inv)
     l1[b] = square
     losses = exchange(lambda p: l1.at[b], lambda me: l1.at[me], "seq", n_seq, b, seq_send.at[3], seq_recv.at[3])
     start(losses)
+    for h in range(heads_dev):
+        normed, gate = inner[h], gate_acc[:, h * hd:(h + 1) * hd]
+        grad_gated = scale * (mask_col[...] * (normed * gate - head(tb, h).astype(F32)))
+        dn = grad_gated * gate
+        product = jnp.mean(dn * normed, axis=-1, keepdims=True)
+        gout[h] = (invs[h] * (dn - normed * product)).astype(BF16)
+        ggate_ref[0, :, h * hd:(h + 1) * hd] = (dn * normed * (1.0 - gate)).astype(BF16)
     pack(g1src, [
         functools.reduce(jnp.add, [mm(part, gout[h], TN) for part in split(head(qb, h).astype(F32) * opening[h])])
         for h in range(heads_dev)
@@ -294,6 +315,8 @@
         gvp[h] = mm(pbuf[h], grad, TN)
     arrived(losses)
     l2[x] = functools.reduce(jnp.add, [l1[j] for j in range(n_seq)])
+    for copies in (*ring, *share, *step_y, *relay, infos, states, counts, states_in):
+        sent(copies)
     losses_dp = exchange(lambda p: l2.at[x], lambda me: l2.at[me], "dp", n_dp, x, dp_send.at[1], dp_recv.at[1])
     start(losses_dp)
     arrived(grads)
@@ -306,6 +329,7 @@
     pl.semaphore_wait(ready.at[2], 2)
     losses_z = exchange(lambda p: l3.at[z], lambda me: l3.at[me], "heads", n_heads, z, z_send, z_recv)
     start(losses_z)
+    sent(grads)
     arrived(states_after)
     for h in range(heads_dev):
         after = unpack(g2, h)
@@ -313,15 +337,16 @@
         gv_ref[0, :, h * hd:(h + 1) * hd] = (gvp[h] + closing[h] * times(head(kb, h), after)).astype(BF16)
     arrived(losses_z)
     total = functools.reduce(jnp.add, [l3[j] for j in range(n_heads)])
-    loss_ref[0, 0] = jnp.sum(total / (2.0 * count * (heads_dev * n_heads * hd)))
-
-    for copies in (to_ahead, to_back, onward, *passes, infos, states, counts, states_in, losses, grads, losses_dp, states_after, losses_z):
+    loss_ref[...] = total / (2.0 * count * (heads_dev * n_heads * hd))
+    for copies in (losses, losses_dp, states_after, losses_z):
         sent(copies)
 
 
 def deliver(*refs):
-    *arrays, sems = refs
-    copies = [pltpu.make_async_copy(arrays[i], arrays[i + 5], sems.at[i]) for i in range(5)]
+    *arrays, loss, sems = refs
+    loss[0, 0] = jnp.sum(arrays[5][...])
+    arrays[5] = loss
+    copies = [pltpu.make_async_copy(arrays[i], arrays[i + 6], sems.at[i]) for i in range(6)]
     start(copies)
     for copy in copies:
         copy.wait()
@@ -339,38 +364,38 @@
     held = pltpu.VMEM((1, T, width), BF16)
     state = pltpu.VMEM((n_seq, heads_dev * rows, hd), STATE)
     scratch = [
+        pltpu.SMEM((heads_dev,), jnp.int32),
         pltpu.VMEM((T, D), BF16), pltpu.VMEM((n_dp, depth, width), BF16),
         *[pltpu.VMEM((T, width), BF16)] * 4,
         pltpu.VMEM((1, T), jnp.int32), pltpu.VMEM((1, T), jnp.int32), pltpu.VMEM((T, width), F32), pltpu.VMEM((T, hd), F32),
         pltpu.VMEM((heads_dev, T, T), F32), pltpu.VMEM((heads_dev, T, T), BF16),
         pltpu.VMEM((heads_dev, T, hd), F32), pltpu.VMEM((heads_dev, T, hd), F32), pltpu.VMEM((heads_dev, T, hd), F32),
         pltpu.VMEM((heads_dev, T, hd), BF16), pltpu.VMEM((heads_dev, T, hd), F32), pltpu.VMEM((heads_dev, T, hd), F32),
-        pltpu.VMEM((n_seq, 8, hd), F32), pltpu.VMEM((n_dp, 4, hd), F32),
-        pltpu.VMEM((n_seq, 8, hd), F32), pltpu.VMEM((n_dp, 8, hd), F32), pltpu.VMEM((n_heads, 8, hd), F32),
+        pltpu.VMEM((n_seq, 2, hd), F32), pltpu.VMEM((n_dp, 1, hd), F32),
+        pltpu.VMEM((n_seq, 1, hd), F32), pltpu.VMEM((n_dp, 1, hd), F32), pltpu.VMEM((n_heads, 1, hd), F32),
         *[state] * 8,
-        pltpu.SemaphoreType.DMA((8,)),
-        pltpu.SemaphoreType.DMA((3, CHUNKS)), pltpu.SemaphoreType.DMA((3, CHUNKS)),
-        pltpu.SemaphoreType.DMA((3, CHUNKS)), pltpu.SemaphoreType.DMA((3, CHUNKS)),
+        pltpu.SemaphoreType.DMA((9,)),
+        pltpu.SemaphoreType.DMA((4, 3, CHUNKS)), pltpu.SemaphoreType.DMA((4, 3, CHUNKS)),
         pltpu.SemaphoreType.DMA((6, n_seq)), pltpu.SemaphoreType.DMA((6, n_seq)),
         pltpu.SemaphoreType.DMA((2, n_dp)), pltpu.SemaphoreType.DMA((2, n_dp)),
         pltpu.SemaphoreType.DMA((n_heads,)), pltpu.SemaphoreType.DMA((n_heads,)), pltpu.SemaphoreType.REGULAR((3,)),
     ]
-    vmem, smem = pl.BlockSpec(memory_space=pltpu.VMEM), pl.BlockSpec(memory_space=pltpu.SMEM)
-    *results, loss = pl.pallas_call(
+    vmem = pl.BlockSpec(memory_space=pltpu.VMEM)
+    results = pl.pallas_call(
         functools.partial(kernel, n_dp, n_seq, n_heads),
-        out_shape=[held] * 5 + [jax.ShapeDtypeStruct((1, 1), F32)],
-        in_specs=[smem] + [any_spec] * 8,
-        out_specs=[vmem] * 5 + [smem],
+        out_shape=[held] * 5 + [pltpu.VMEM((1, hd), F32)],
+        in_specs=[any_spec] * 9,
+        out_specs=[vmem] * 6,
         scratch_shapes=scratch,
         compiler_params=pltpu.CompilerParams(collective_id=0, has_side_effects=True),
         name="layer",
     )(decay_index, loss_mask, doc_reset, hidden, w_gate, query_rows, key_rows, value_rows, target)
-    results = pl.pallas_call(
+    *results, loss = pl.pallas_call(
         deliver,
-        out_shape=[out] * 5,
-        in_specs=[vmem] * 5,
-        out_specs=[any_spec] * 5,
-        scratch_shapes=[pltpu.SemaphoreType.DMA((5,))],
+        out_shape=[out] * 5 + [jax.ShapeDtypeStruct((1, 1), F32)],
+        in_specs=[vmem] * 6,
+        out_specs=[any_spec] * 6,
+        scratch_shapes=[pltpu.SMEM((1, 1), F32), pltpu.SemaphoreType.DMA((6,))],
         name="deliver",
     )(*[pltpu.with_memory_space_constraint(r, pltpu.VMEM) for r in results])
     return (*results, loss.reshape(()))

time: 59.1 us -> 55.6 us (0.941)
  Pallas kernels: 56.5 us -> 54.3 us
  between operations: 2.41 us -> 0.64 us
    pallas_call x1, Pallas kernels: 55.7 us -> 53.5 us  [local_step(): pl.pallas_call(functools.partial(kernel, n_dp, n_seq, n_heads), out_shape...]
where the time goes in v4:
time: 55.6 us; the launch traced here: 55 us
  Pallas kernels  54.3 us (98%)
  between operations  0.64 us (1%)
    pallas_call x1, Pallas kernels, local_step(): pl.pallas_call(functools.partial(kernel, n_dp, n_seq, n_heads), out_shape...  53.5 us

profile of v4, /device:TPU:1, one launch (start us, length us, event | category | flops | bytes accessed | tf_op | source)
XLA Modules:
  0.0 55.0 jit_solution(9512928499224874375)
XLA Ops:
  0.6 53.5 %layer.1 = (bf16[1,256,256]{2,1,0:T(8,128)(2,1)S(1)}, bf16[1,256,256]{2,1,0:T(8,128)(2,1)S(1)}, bf16[1,256,256]{2,1,0:T(8,128)(2,1)S(1)}, bf16[1,256,256]{2,1,0:...) custom-call(s32[2]{0:T(128)} %idx_hbm.1, s32[1,256]{1,0:T(1,128)} %mask_hbm.1, ...), custom_call_target="tpu_custom_call" | custom-call | tf_op jit(solution)/shard_map/layer/pallas_call | solution.py:384
  54.1 0.9 %deliver.1 = (bf16[1,256,256]{2,1,0:T(8,128)(2,1)}, bf16[1,256,256]{2,1,0:T(8,128)(2,1)}, bf16[1,256,256]{2,1,0:T(8,128)(2,1)}, bf16[1,256,256]{2,1,0:T(8,128)(2...) custom-call(bf16[1,256,256]{2,1,0:T(8,128)(2,1)S(1)} %get-tuple-element.18.refs_0_, ...), custom_call_target="tpu_custom_call" | custom-call | tf_op jit(solution)/shard_map/deliver/pallas_call | solution.py:393

commit v5 on v4

--- a/solution.py
+++ b/solution.py
@@ -10,7 +10,7 @@
 
 TABLE = 16
 NORM_EPS = 1e-06
-CHUNKS = 3
+SHARED, ALONE = 1, 2
 STATE = jnp.bfloat16
 F32, BF16 = jnp.float32, jnp.bfloat16
 NN, NT, TN = ((1,), (0,)), ((1,), (1,)), ((0,), (0,))
@@ -79,7 +79,7 @@
     hd = gout.shape[2]
     heads_dev = gout.shape[0]
     depth = w_hbm.shape[0]
-    piece = depth // 4 // CHUNKS
+    piece = depth // (4 * SHARED + 2 * ALONE)
     rows = hd // n_seq
     core = lax.rem(b, 2)
     sibling = b + 1 - 2 * core
@@ -160,18 +160,20 @@
 
     wave_signal(1, 0)
 
-    def w_piece(shard, part, i):
-        return wbuf.at[shard, pl.ds(pl.multiple_of(part * (depth // 4) + i * piece, piece), piece), :]
+    def w_rows(part, i):
+        first = part * SHARED + i if i < SHARED else 4 * SHARED + core * ALONE + i - SHARED
+        return pl.ds(pl.multiple_of(first * piece, piece), piece)
 
     def w_copy(kind, route, shard, part, i, target, src=None):
+        rows_at = wbuf.at[shard, w_rows(part, i), :]
         return pltpu.make_async_remote_copy(
-            src_ref=w_piece(shard, part, i) if src is None else src, dst_ref=w_piece(shard, part, i),
+            src_ref=rows_at if src is None else src, dst_ref=rows_at,
             send_sem=w_send.at[kind, route, i], recv_sem=w_recv.at[kind, route, i],
             device_id=target, device_id_type=pl.DeviceIdType.MESH,
         )
 
-    steps = range(CHUNKS)
-    own = [w_hbm.at[pl.ds(pl.multiple_of(quarter * (depth // 4) + i * piece, piece), piece), :] for i in steps]
+    steps, shared = range(SHARED + ALONE), range(SHARED)
+    own = [w_hbm.at[w_rows(quarter, i), :] for i in steps]
     shards = (back, ahead, across)
     ring = [
         [w_copy(0, 0, x, quarter, i, {"dp": ahead}, own[i]) for i in steps],
@@ -179,14 +181,15 @@
         [w_copy(0, 2, back, quarter, i, {"dp": ahead}) for i in steps],
     ]
     share = [[w_copy(1, r, shards[r], quarter, i, {"seq": sibling}) for i in steps] for r in range(3)]
-    step_y = [[w_copy(2, r, shards[r], quarter, i, {"seq": beside}) for i in steps] for r in range(3)]
-    relay = [[w_copy(3, r, shards[r], other, i, {"seq": sibling}) for i in steps] for r in range(3)]
+    step_y = [[w_copy(2, r, shards[r], quarter, i, {"seq": beside}) for i in shared] for r in range(3)]
+    relay = [[w_copy(3, r, shards[r], other, i, {"seq": sibling}) for i in shared] for r in range(3)]
 
     def from_ring(r, i):
         ring[r][i].wait_recv()
         if r == 0:
             ring[2][i].start()
-        step_y[r][i].start()
+        if i < SHARED:
+            step_y[r][i].start()
         share[r][i].start()
 
     def from_side(r, i):
@@ -241,7 +244,7 @@
             result[j] = state.astype(result.dtype)
             state = carry * keep[j] * state + source[j].astype(F32)
 
-    for i in steps[1:-1]:
+    for i in steps[1:SHARED]:
         from_ring(0, i)
         from_ring(1, i)
     arrived(states)
@@ -249,21 +252,26 @@
     states_in = exchange(lambda p: s2src.at[p], lambda me: s2.at[me], "seq", n_seq, b, seq_send.at[2], seq_recv.at[2])
     start(states_in)
     s2[b] = s2src[b]
-    from_ring(0, CHUNKS - 1)
-    from_ring(1, CHUNKS - 1)
+    from_ring(0, SHARED)
+    from_ring(1, SHARED)
     local[8].wait()
     pl.semaphore_wait(ready.at[1], 2)
     wave_signal(4, 2)
-    for i in steps:
+    for i in shared:
         from_side(0, i)
         from_side(1, i)
+        from_ring(2, i)
+    for i in steps[SHARED + 1:]:
+        from_ring(0, i)
+        from_ring(1, i)
+    for i in shared:
+        from_side(2, i)
+    for i in steps[SHARED:]:
         from_ring(2, i)
     for copies in (*share[:2], *relay[:2]):
         arrived(copies)
     gate_part(back)
     gate_part(ahead)
-    for i in steps:
-        from_side(2, i)
     arrived(states_in)
     state_in = [unpack(s2, h) for h in range(heads_dev)]
     for h in range(heads_dev):
@@ -315,10 +323,10 @@
         gvp[h] = mm(pbuf[h], grad, TN)
     arrived(losses)
     l2[x] = functools.reduce(jnp.add, [l1[j] for j in range(n_seq)])
+    losses_dp = exchange(lambda p: l2.at[x], lambda me: l2.at[me], "dp", n_dp, x, dp_send.at[1], dp_recv.at[1])
+    start(losses_dp)
     for copies in (*ring, *share, *step_y, *relay, infos, states, counts, states_in):
         sent(copies)
-    losses_dp = exchange(lambda p: l2.at[x], lambda me: l2.at[me], "dp", n_dp, x, dp_send.at[1], dp_recv.at[1])
-    start(losses_dp)
     arrived(grads)
     scan(g1, g2src, range(n_seq - 1, -1, -1))
     states_after = exchange(lambda p: g2src.at[p], lambda me: g2.at[me], "seq", n_seq, b, seq_send.at[5], seq_recv.at[5])
@@ -375,7 +383,7 @@
         pltpu.VMEM((n_seq, 1, hd), F32), pltpu.VMEM((n_dp, 1, hd), F32), pltpu.VMEM((n_heads, 1, hd), F32),
         *[state] * 8,
         pltpu.SemaphoreType.DMA((9,)),
-        pltpu.SemaphoreType.DMA((4, 3, CHUNKS)), pltpu.SemaphoreType.DMA((4, 3, CHUNKS)),
+        pltpu.SemaphoreType.DMA((4, 3, SHARED + ALONE)), pltpu.SemaphoreType.DMA((4, 3, SHARED + ALONE)),
         pltpu.SemaphoreType.DMA((6, n_seq)), pltpu.SemaphoreType.DMA((6, n_seq)),
         pltpu.SemaphoreType.DMA((2, n_dp)), pltpu.SemaphoreType.DMA((2, n_dp)),
         pltpu.SemaphoreType.DMA((n_heads,)), pltpu.SemaphoreType.DMA((n_heads,)), pltpu.SemaphoreType.REGULAR((3,)),

time: 55.6 us -> 53.9 us (0.969)
  Pallas kernels: 54.3 us -> 52.6 us
    pallas_call x1, Pallas kernels: 53.5 us -> 51.7 us  [local_step(): pl.pallas_call(functools.partial(kernel, n_dp, n_seq, n_heads), out_shape...]
where the time goes in v5:
time: 53.9 us; the launch traced here: 53.2 us
  Pallas kernels  52.6 us (98%)
  between operations  0.64 us (1%)
    pallas_call x1, Pallas kernels, local_step(): pl.pallas_call(functools.partial(kernel, n_dp, n_seq, n_heads), out_shape...  51.7 us

profile of v5, /device:TPU:1, one launch (start us, length us, event | category | flops | bytes accessed | tf_op | source)
XLA Modules:
  0.0 53.2 jit_solution(14261187211751137376)
XLA Ops:
  0.6 51.7 %layer.1 = (bf16[1,256,256]{2,1,0:T(8,128)(2,1)S(1)}, bf16[1,256,256]{2,1,0:T(8,128)(2,1)S(1)}, bf16[1,256,256]{2,1,0:T(8,128)(2,1)S(1)}, bf16[1,256,256]{2,1,0:...) custom-call(s32[2]{0:T(128)} %idx_hbm.1, s32[1,256]{1,0:T(1,128)} %mask_hbm.1, ...), custom_call_target="tpu_custom_call" | custom-call | tf_op jit(solution)/shard_map/layer/pallas_call | solution.py:392
  52.3 0.9 %deliver.1 = (bf16[1,256,256]{2,1,0:T(8,128)(2,1)}, bf16[1,256,256]{2,1,0:T(8,128)(2,1)}, bf16[1,256,256]{2,1,0:T(8,128)(2,1)}, bf16[1,256,256]{2,1,0:T(8,128)(2...) custom-call(bf16[1,256,256]{2,1,0:T(8,128)(2,1)S(1)} %get-tuple-element.18.refs_0_, ...), custom_call_target="tpu_custom_call" | custom-call | tf_op jit(solution)/shard_map/deliver/pallas_call | solution.py:401
